TPU v7x, 32 devices: a whole 2x2x4 slice. The times are simulated.
32 devices in a mesh: parts: 2 (over x), xy: 16 (over z, y, core).
Axes of the slice: x: 2, y: 2, z: 4, core: 2. Of those that a mesh axis runs over, the one named last changes fastest.
Arguments:
- affinity: bfloat16 [3, 256, 64, 128], P(None, ('parts', 'xy')), parts along dimension 1, may hold values from 0 to 1
- block_scale: float32 [3, 256, 64], P(None, ('parts', 'xy')), parts along dimension 1, may hold values from 0.5 to 2
- slot_map: int32 [256, 64, 128], P(('parts', 'xy')), parts along dimension 0, may hold values from 0 to 7, as said below
- edge_list: int32 [256, 64, 8], P(('parts', 'xy')), parts along dimension 0, may hold values from 0 to 8191, as said below
- valid_count: int32 [256, 64], P(('parts', 'xy')), parts along dimension 0, may hold values from 5 to 8
- edge_home: int32 [16384], P('parts'), parts along dimension 0, may hold values from 0 to 8191, as said below
Outputs:
- edge_features: float32 [16384, 64], P(('parts', 'xy')), parts along dimension 0
There are 2 independent parts, one for each index of `parts`. A program takes and returns all parts, laid end to end along the dimension named above; each array names one. Nothing has to cross between parts.
Inputs may be any that keep to these rules, and one draw needn't show every extreme that they name: `slot_map`: every voxel's entry is below its block's valid_count. `edge_list`: among the used entries of the blocks of one device (8 planes), at most 512 name edges whose edge_home lies in any one range [k * 512, (k + 1) * 512); in every draw some range receives exactly 512 from every device. `edge_home`: a permutation of 0 to 8191.
All inputs are finite; a program needn't handle non-finite values.
Results may differ from a plain program's by a relative error of at most 0.0003.
Values sent between devices are 32-bit elements; how exact they have to be, the bound alone decides.
No kernel may reach another device: no remote copies, remote signals or barrier semaphores. Data moves between devices by JAX's collectives and lax.ppermute only.
A program may use at most 64 MiB of HBM per device.

v0:
```python
import functools

import jax
import jax.numpy as jnp
import numpy as np
from jax import lax
from jax.experimental import pallas as pl
from jax.experimental.pallas import tpu as pltpu
from jax.sharding import PartitionSpec as P

SLOTS = 8
HALO = 8
FEAT = 64
LANES = 128

sigma_list = (0.8, 1.3, 2.0, 3.0)
SCALES = len(sigma_list)
RESP = 3 * SCALES
ROWS = 2 * RESP + 2 * RESP + 8


def taps(sigma):
    offsets = np.arange(-HALO, HALO + 1).astype(np.float32)
    weights = np.exp(-offsets * offsets / np.float32(2.0 * sigma * sigma)).astype(np.float32)
    return (weights / weights.sum(dtype=np.float32)).astype(np.float32)


def band(weights, length):
    rows = np.arange(length)[:, None]
    cols = np.arange(length)[None, :]
    offset = cols - rows + HALO
    inside = (offset >= 0) & (offset <= 2 * HALO)
    return np.where(inside, weights[np.clip(offset, 0, 2 * HALO)], 0.0).astype(np.float32)


def halves(value):
    high = value.astype(jnp.bfloat16)
    low = (value - high.astype(jnp.float32)).astype(jnp.bfloat16)
    return high, low


def constant_halves(value):
    high = value.astype(jnp.bfloat16)
    low = (value - high.astype(np.float32)).astype(jnp.bfloat16)
    return high, low


def filter_constants(height, depth):
    along_y, along_z = [], []
    for sigma in sigma_list:
        high, low = constant_halves(band(taps(sigma), depth).T)
        along_y.append(np.concatenate([high, high, low], 0))
        high, low = constant_halves(band(taps(sigma), height))
        along_z.append(np.concatenate([high, high, low], 1))
    return np.stack(along_y), np.stack(along_z)


def column_constants():
    columns = np.arange(LANES)
    block = np.where(columns < 120, columns % 24 // 12, (columns - 120) // 4)
    feature = np.where(columns < 120, columns // 24 * 12 + columns % 12, 60 + columns % 4)
    place = np.zeros((LANES, 2 * LANES), np.float32)
    place[columns, feature] = 1.0
    place[columns, LANES + FEAT + feature] = 1.0
    keep = (np.repeat(np.arange(2), SLOTS)[:, None] == block[None, :]).astype(np.float32)
    return np.concatenate([place, place], 0).astype(jnp.bfloat16), keep


def order_bits(owners):
    bits = owners.bit_length() - 1
    first = list(range(bits))
    return first, [0] + first[2:] + first[1:2]


def index_kernel(owners, rows_owned, height, me_ref, edge_ref, count_ref, home_ref, target_ref, source_ref):
    lists = edge_ref[...]
    both = jnp.concatenate([lists, lists], 1)
    high = both // LANES
    low = both % LANES

    def pick(row, found):
        line = jnp.broadcast_to(home_ref[pl.ds(row, 1), :], both.shape)
        return jnp.where(high == row, jnp.take_along_axis(line, low, axis=1), found)

    home = lax.fori_loop(0, home_ref.shape[0], pick, jnp.zeros(both.shape, jnp.int32))[:, :height]
    entry = lax.broadcasted_iota(jnp.int32, home.shape, 0)
    slot = entry % SLOTS
    plane = entry // SLOTS
    column = lax.broadcasted_iota(jnp.int32, home.shape, 1)
    half = height // 2
    number = ((plane * half + column % half) * 2 + column // half) * SLOTS + slot
    owner = (home // rows_owned) ^ me_ref[0]
    within = home % rows_owned
    quarter = rows_owned // 4
    part = within // (2 * quarter)
    first, second = order_bits(owners)
    bits = len(first)
    place_first = jnp.zeros_like(owner)
    place_second = jnp.zeros_like(owner)
    for position in range(bits):
        place_first += ((owner >> first[position]) & 1) << (bits - 1 - position)
        place_second += ((owner >> second[position]) & 1) << (bits - 1 - position)
    place = jnp.where(part == 0, place_first, owners + place_second)
    row = place * quarter + within % quarter
    side = (within // quarter) % 2
    valid = slot < count_ref[...]
    target_ref[...] = jnp.where(valid, row, 2 * owners * quarter)
    source_ref[...] = side * (entry.shape[0] * height) + number


def main_kernel(
    copies, before_ref, own_ref, after_ref, slots_ref, y_ref, z_ref, place_ref, keep_ref, target_ref, source_ref,
    first_ref, second_ref, *scratch,
):
    blurred, fields, entries = scratch[:3]
    tables = scratch[3:]
    planes, height, depth = own_ref.shape[1:]
    half = height // 2
    weights = [[float(w) for w in taps(sigma)] for sigma in sigma_list]

    for table in tables:
        def clear(step, carry, table=table):
            table[pl.ds(pl.multiple_of(step * 64, 64), 64), :] = jnp.zeros((64, LANES), jnp.float32)
            return carry
        lax.fori_loop(0, table.shape[0] // 64, clear, 0)

    tiles = height // 8

    def across(step, carry):
        channel = step // tiles
        rows = pl.ds(pl.multiple_of(step % tiles * 8, 8), 8)
        values = [before_ref[channel, planes - HALO + p, rows, :] for p in range(HALO)]
        values += [own_ref[channel, p, rows, :] for p in range(planes)]
        values += [after_ref[channel, p, rows, :] for p in range(HALO)]
        for q in range(planes):
            center = q + HALO
            sums = [values[center]] + [values[center - t] + values[center + t] for t in range(1, HALO + 1)]
            for scale in range(SCALES):
                total = sums[0] * weights[scale][HALO]
                for t in range(1, HALO + 1):
                    total = total + sums[t] * weights[scale][HALO + t]
                blurred[scale * 3 + channel, q, rows, :] = total
        return carry

    lax.fori_loop(0, 3 * tiles, across, 0)

    def put(row, value):
        for q in range(planes):
            for b in range(2):
                start = q * half * ROWS + row + b * (RESP if row < 4 * RESP else 4)
                fields[pl.ds(start, half, stride=ROWS), :] = value[b * half : (b + 1) * half, q * LANES : (q + 1) * LANES]

    for scale in range(SCALES):
        results = []
        for channel in range(3):
            high, low = halves(blurred[scale * 3 + channel].reshape(planes * height, depth))
            line = jnp.dot(jnp.concatenate([high, low, high], 1), y_ref[scale], preferred_element_type=jnp.float32)
            high, low = halves(line)
            stacked = jnp.concatenate([high.reshape(planes, height, depth), low.reshape(planes, height, depth), high.reshape(planes, height, depth)], 1)
            side_by_side = jnp.concatenate([stacked[q] for q in range(planes)], 1)
            result = jnp.dot(z_ref[scale], side_by_side, preferred_element_type=jnp.float32)
            put(scale * 3 + channel, result)
            results.append(result)
        for number, (a, b) in enumerate(((0, 1), (0, 2), (1, 2))):
            put(2 * RESP + scale * 3 + number, results[a] * results[b])
    for channel in range(3):
        put(4 * RESP + channel, jnp.concatenate([own_ref[channel, q] for q in range(planes)], 1))
    put(4 * RESP + 3, jnp.ones((height, planes * LANES), jnp.float32))

    sub = lax.broadcasted_iota(jnp.int32, (SLOTS, LANES), 0)
    keep = keep_ref[...]
    place = place_ref[...]
    group = 8
    entry_count = planes * height * SLOTS

    def block_sums(step, carry):
        plane = step // (half // group)
        base = step % (half // group) * group
        parts = []
        for g in range(group):
            zz = base + g
            tile = fields[pl.ds(pl.multiple_of((plane * half + zz) * ROWS, 8), ROWS), :]
            resp = tile[: 2 * RESP]
            square = resp * resp
            feats = jnp.concatenate(
                [resp, square, square * resp, square * square, tile[2 * RESP :]], 0
            )
            high, low = halves(feats)
            upper = (slots_ref[plane, pl.ds(zz, 1), :] == sub).astype(jnp.float32)
            lower = (slots_ref[plane, pl.ds(zz + half, 1), :] == sub).astype(jnp.float32)
            hot = jnp.concatenate([upper, lower], 0).astype(jnp.bfloat16)
            dims = (((1,), (1,)), ((), ()))
            sums = lax.dot_general(
                jnp.concatenate([hot, hot], 1), jnp.concatenate([high, low], 1), dims, preferred_element_type=jnp.float32
            )
            parts.append(sums * keep)
        high, low = halves(jnp.concatenate(parts, 0))
        placed = jnp.dot(jnp.concatenate([high, low], 1), place, preferred_element_type=jnp.float32)
        start = pl.multiple_of(step * (group * 2 * SLOTS), group * 2 * SLOTS)
        entries[pl.ds(start, group * 2 * SLOTS), :] = placed[:, :LANES]
        entries[pl.ds(entry_count + start, group * 2 * SLOTS), :] = placed[:, LANES:]
        return carry

    lax.fori_loop(0, planes * half // group, block_sums, 0)

    def scatter(step, carry):
        row = step // (height // 16)
        first = step % (height // 16) * 16
        for offset in range(0, 16, copies):
            for number, table in enumerate(tables):
                column = first + offset + number
                target = target_ref[row, column]
                source = source_ref[row, column]
                table[pl.ds(target, 1), :] = table[pl.ds(target, 1), :] + entries[pl.ds(source, 1), :]
        return carry

    lax.fori_loop(0, planes * SLOTS * (height // 16), scatter, 0)

    length = first_ref.shape[0]

    def combine(step, carry):
        for out, offset in ((first_ref, 0), (second_ref, length)):
            start = pl.multiple_of(step * 64, 64)
            total = tables[0][pl.ds(offset + start, 64), :]
            for table in tables[1:]:
                total = total + table[pl.ds(offset + start, 64), :]
            out[pl.ds(start, 64), :] = total
        return carry

    lax.fori_loop(0, length // 64, combine, 0)


def final_kernel(first_keep, first_got, second_keep, second_got, out_ref):
    quarter = first_keep.shape[0]
    for number, (keep, got) in enumerate(((first_keep, first_got), (second_keep, second_got))):
        table = keep[...] + got[...]
        for side in range(2):
            rows = table[:, side * FEAT : (side + 1) * FEAT]
            count = rows[:, FEAT - 1 : FEAT]
            lane = lax.broadcasted_iota(jnp.int32, rows.shape, 1)
            means = rows / jnp.maximum(count, 1.0)
            result = jnp.where(lane == FEAT - 1, jnp.log(1.0 + rows), means)
            out_ref[pl.ds((2 * number + side) * quarter, quarter), :] = result


def shards(affinity, block_scale, slot_map, edge_list, valid_count, edge_home):
    planes, height, depth = affinity.shape[1:]
    owners = lax.axis_size("xy")
    rows_owned = edge_home.shape[0] // owners
    quarter = rows_owned // 4
    vmem = pl.BlockSpec(memory_space=pltpu.VMEM)
    smem = pl.BlockSpec(memory_space=pltpu.SMEM)

    dequant = affinity.astype(jnp.float32) * block_scale[..., None]
    up = [(i, i + 1) for i in range(owners - 1)]
    down = [(j, i) for i, j in up]
    before = lax.ppermute(dequant[:, planes - HALO :], "xy", up)
    after = lax.ppermute(dequant[:, :HALO], "xy", down)

    me = lax.axis_index("xy").astype(jnp.int32).reshape(1)
    lists = edge_list.transpose(0, 2, 1).reshape(planes * SLOTS, height)
    counts = jnp.broadcast_to(valid_count[:, None, :], (planes, SLOTS, height)).reshape(planes * SLOTS, height)
    index_shape = jax.ShapeDtypeStruct((planes * SLOTS, height), jnp.int32)
    target, source = pl.pallas_call(
        functools.partial(index_kernel, owners, rows_owned, height),
        out_shape=(index_shape, index_shape),
        in_specs=[smem, vmem, vmem, vmem],
        out_specs=(vmem, vmem),
        name="index",
    )(me, lists, counts, edge_home.reshape(-1, LANES))

    along_y, along_z = filter_constants(height, depth)
    place, keep = column_constants()
    table_rows = 2 * owners * quarter
    copies = 4 if table_rows <= 4096 else 2
    table_shape = jax.ShapeDtypeStruct((owners * quarter, LANES), jnp.float32)
    entry_count = planes * height * SLOTS
    first, second = pl.pallas_call(
        functools.partial(main_kernel, copies),
        out_shape=(table_shape, table_shape),
        in_specs=[vmem] * 8 + [smem, smem],
        out_specs=(vmem, vmem),
        scratch_shapes=[
            pltpu.VMEM((RESP, planes, height, depth), jnp.float32),
            pltpu.VMEM((planes * (height // 2) * ROWS, LANES), jnp.float32),
            pltpu.VMEM((2 * entry_count, LANES), jnp.float32),
        ]
        + [pltpu.VMEM((table_rows + 64, LANES), jnp.float32)] * copies,
        compiler_params=pltpu.CompilerParams(vmem_limit_bytes=56 << 20),
        name="features",
    )(before, dequant, after, slot_map, jnp.asarray(along_y), jnp.asarray(along_z), jnp.asarray(place), jnp.asarray(keep), target, source)

    order_first, order_second = order_bits(owners)

    def exchange(value, bit):
        middle = value.shape[0] // 2
        pairs = [(i, i ^ (1 << bit)) for i in range(owners)]
        return value[:middle], lax.ppermute(value[middle:], "xy", pairs)

    for stage in range(len(order_first)):
        first_pair = exchange(first, order_first[stage])
        second_pair = exchange(second, order_second[stage])
        if stage < len(order_first) - 1:
            first = first_pair[0] + first_pair[1]
            second = second_pair[0] + second_pair[1]
    return pl.pallas_call(
        final_kernel,
        out_shape=jax.ShapeDtypeStruct((rows_owned, FEAT), jnp.float32),
        in_specs=[vmem] * 4,
        out_specs=vmem,
        name="final",
    )(*first_pair, *second_pair)


def solution(mesh):
    in_specs = (
        P(None, ("parts", "xy"), None, None),
        P(None, ("parts", "xy"), None),
        P(("parts", "xy"), None, None),
        P(("parts", "xy"), None, None),
        P(("parts", "xy"), None),
        P("parts"),
    )
    out_specs = P(("parts", "xy"), None)
    return jax.shard_map(shards, mesh=mesh, in_specs=in_specs, out_specs=out_specs, check_vma=False)
```

profile of v0, /device:TPU:0, one launch (start us, length us, event | category | flops | bytes accessed | tf_op | source)
XLA Modules:
  0.0 97.6 jit_solution(17375105331500639218)
XLA Ops:
  0.0 1.3 %convert_multiply_fusion.own_ref = f32[3,8,64,128]{3,2,1,0:T(8,128)S(1)} fusion(bf16[3,8,64,128]{3,2,1,0:T(8,128)(2,1)} %param.10, f32[3,8,64]{2,1,0:T(8,128)} %param.11), kind=kLoop, calls=%fused_computation | loop fusion | flops 393216 | bytes 1185792 | tf_op jit(solution)/shard_map/mul | solution.py:254
  1.3 1.3 %collective-permute-start.1 = (f32[3,8,64,128]{3,2,1,0:T(8,128)S(1)}, f32[3,8,64,128]{3,2,1,0:T(8,128)S(1)}, u32[]{:S(2)}, u32[]{:S(2)}) collective-permute-start(f32[3,8,64,128]{3,2,1,0:T(8,128)S(1)} %convert_multiply_fusion.own_ref), channel_id=1, source_target_pairs={{1,0},{2,1},{3,2},{4,3},{5,4},{6,5},{7,6},{8,7},{9,8},{10,9},{11,1... | collective-permute-start | bytes 2359304 | tf_op jit(solution)/shard_map/ppermute | solution.py:258
  2.6 3.1 %collective-permute-start = (f32[3,8,64,128]{3,2,1,0:T(8,128)S(1)}, f32[3,8,64,128]{3,2,1,0:T(8,128)S(1)}, u32[]{:S(2)}, u32[]{:S(2)}) collective-permute-start(f32[3,8,64,128]{3,2,1,0:T(8,128)S(1)} %convert_multiply_fusion.own_ref), channel_id=1, source_target_pairs={{0,1},{1,2},{2,3},{3,4},{4,5},{5,6},{6,7},{7,8},{8,9},{9,10},{10,1... | collective-permute-start | bytes 2359304 | tf_op jit(solution)/shard_map/ppermute | solution.py:257
  5.7 0.6 broadcast_bitcast_fusion.count_ref
  6.3 7.3 %index.1 = (s32[64,64]{1,0:T(8,128)}, s32[64,64]{1,0:T(8,128)}) custom-call(s32[1]{0:T(128)} %bitcast.me_ref, s32[64,64]{1,0:T(8,128)} %bitcast.7, s32[64,64]{1,0:T(8,128)} %broadcast_bitcast_fusion.count_ref, s32[64,128]{1,0:T(8,128)} %bitcast.8), custom_call_target="tpu_custom_call" | custom-call | tf_op jit(solution)/shard_map/index/pallas_call | solution.py:264
  13.6 0.0 collective-permute-done.1.after_ref
  13.6 0.0 collective-permute-done.before_ref
  13.7 0.9 copy-done.4
  14.5 0.2 copy-done.5
  14.8 38.5 %features.1 = (f32[2048,128]{1,0:T(8,128)}, f32[2048,128]{1,0:T(8,128)}) custom-call(f32[3,8,64,128]{3,2,1,0:T(8,128)} %copy-done.5, f32[3,8,64,128]{3,2,1,0:T(8,128)} %copy-done.1, f32[3,8,64,128]{3,2,1,0:T(8,128)} %copy-done.4, s32[8,64,128]{2,1,0:T(8,128)} %slots_ref.1, bf16[4,384,128]{2,1,0:T(8,128)(2,1)} %constant.12.clone.y_ref, ...), custom_call_target="tpu_custom_call" | custom-call | tf_op jit(solution)/shard_map/features/pallas_call | solution.py:278
  53.2 1.2 %slice.57 = f32[1024,128]{1,0:T(8,128)S(1)} slice(f32[2048,128]{1,0:T(8,128)} %get-tuple-element.12), slice={[1024:2048], [0:128]} | slice | bytes 1048576 | tf_op jit(solution)/shard_map/slice | solution.py:298
  54.5 10.7 %collective-permute-start.6 = (f32[1024,128]{1,0:T(8,128)S(1)}, f32[1024,128]{1,0:T(8,128)S(1)}, u32[]{:S(2)}, u32[]{:S(2)}) collective-permute-start(f32[1024,128]{1,0:T(8,128)S(1)} %slice.57), channel_id=1, source_target_pairs={{0,1},{1,0},{2,3},{3,2},{4,5},{5,4},{6,7},{7,6},{8,9},{9,8},{10,11... | collective-permute-start | bytes 1572872 | tf_op jit(solution)/shard_map/ppermute | solution.py:298
  65.3 0.1 collective-permute-start.2
  65.4 1.4 %collective-permute-done.6 = f32[1024,128]{1,0:T(8,128)S(1)} collective-permute-done((f32[1024,128]{1,0:T(8,128)S(1)}, f32[1024,128]{1,0:T(8,128)S(1)}, u32[]{:S(2)}, u32[]{:S(2)}) %collective-permute-start.6) | collective-permute-done | bytes 524320 | tf_op jit(solution)/shard_map/ppermute | solution.py:298
  66.7 0.1 slice_add_fusion
  66.8 1.8 %collective-permute-start.7 = (f32[512,128]{1,0:T(8,128)S(1)}, f32[512,128]{1,0:T(8,128)S(1)}, u32[]{:S(2)}, u32[]{:S(2)}) collective-permute-start(f32[512,128]{1,0:T(8,128)S(1)} %slice.71), channel_id=1, source_target_pairs={{0,4},{1,5},{2,6},{3,7},{4,0},{5,1},{6,2},{7,3},{8,12},{9,13},{10,... | collective-permute-start | bytes 786440 | tf_op jit(solution)/shard_map/ppermute | solution.py:298
  68.6 0.0 collective-permute-done.2
  68.6 0.1 slice_add_fusion.1
  68.7 2.7 %collective-permute-start.3 = (f32[512,128]{1,0:T(8,128)S(1)}, f32[512,128]{1,0:T(8,128)S(1)}, u32[]{:S(2)}, u32[]{:S(2)}) collective-permute-start(f32[512,128]{1,0:T(8,128)S(1)} %slice.65), channel_id=1, source_target_pairs={{0,2},{1,3},{2,0},{3,1},{4,6},{5,7},{6,4},{7,5},{8,10},{9,11},{10,... | collective-permute-start | bytes 786440 | tf_op jit(solution)/shard_map/ppermute | solution.py:298
  71.4 4.1 %collective-permute-done.7 = f32[512,128]{1,0:T(8,128)S(1)} collective-permute-done((f32[512,128]{1,0:T(8,128)S(1)}, f32[512,128]{1,0:T(8,128)S(1)}, u32[]{:S(2)}, u32[]{:S(2)}) %collective-permute-start.7) | collective-permute-done | bytes 262176 | tf_op jit(solution)/shard_map/ppermute | solution.py:298
  75.5 2.8 %collective-permute-start.8 = (f32[256,128]{1,0:T(8,128)S(1)}, f32[256,128]{1,0:T(8,128)S(1)}, u32[]{:S(2)}, u32[]{:S(2)}) collective-permute-start(f32[256,128]{1,0:T(8,128)S(1)} %slice.73), channel_id=1, source_target_pairs={{0,8},{1,9},{2,10},{3,11},{4,12},{5,13},{6,14},{7,15},{8,0},{9,1},... | collective-permute-start | bytes 393224 | tf_op jit(solution)/shard_map/ppermute | solution.py:298
  78.3 1.6 %collective-permute-start.4 = (f32[256,128]{1,0:T(8,128)S(1)}, f32[256,128]{1,0:T(8,128)S(1)}, u32[]{:S(2)}, u32[]{:S(2)}) collective-permute-start(f32[256,128]{1,0:T(8,128)S(1)} %slice.67), channel_id=1, source_target_pairs={{0,4},{1,5},{2,6},{3,7},{4,0},{5,1},{6,2},{7,3},{8,12},{9,13},{10,... | collective-permute-start | bytes 393224 | tf_op jit(solution)/shard_map/ppermute | solution.py:298
  80.0 4.4 %collective-permute-done.8 = f32[256,128]{1,0:T(8,128)S(1)} collective-permute-done((f32[256,128]{1,0:T(8,128)S(1)}, f32[256,128]{1,0:T(8,128)S(1)}, u32[]{:S(2)}, u32[]{:S(2)}) %collective-permute-start.8) | collective-permute-done | bytes 131104 | tf_op jit(solution)/shard_map/ppermute | solution.py:298
  84.4 0.6 fusion
  85.0 2.1 %collective-permute-start.9 = (f32[128,128]{1,0:T(8,128)S(1)}, f32[128,128]{1,0:T(8,128)S(1)}, u32[]{:S(2)}, u32[]{:S(2)}) collective-permute-start(f32[128,128]{1,0:T(8,128)S(1)} %get-tuple-element.13), channel_id=1, source_target_pairs={{0,2},{1,3},{2,0},{3,1},{4,6},{5,7},{6,4},{7,5},{8,10},{9,11},{10,... | collective-permute-start | bytes 196616 | tf_op jit(solution)/shard_map/ppermute | solution.py:298
  87.2 0.6 fusion.1
  87.8 1.2 %collective-permute-start.5 = (f32[128,128]{1,0:T(8,128)S(1)}, f32[128,128]{1,0:T(8,128)S(1)}, u32[]{:S(2)}, u32[]{:S(2)}) collective-permute-start(f32[128,128]{1,0:T(8,128)S(1)} %get-tuple-element.15), channel_id=1, source_target_pairs={{0,8},{1,9},{2,10},{3,11},{4,12},{5,13},{6,14},{7,15},{8,0},{9,1},... | collective-permute-start | bytes 196616 | tf_op jit(solution)/shard_map/ppermute | solution.py:298
  89.0 0.3 collective-permute-done.9.second_got
  89.4 4.0 %collective-permute-done.5.first_got = f32[128,128]{1,0:T(8,128)S(1)} collective-permute-done((f32[128,128]{1,0:T(8,128)S(1)}, f32[128,128]{1,0:T(8,128)S(1)}, u32[]{:S(2)}, u32[]{:S(2)}) %collective-permute-start.5) | collective-permute-done | bytes 65568 | tf_op jit(solution)/shard_map/ppermute | solution.py:298
  93.4 0.6 copy-done.7
  94.0 1.9 %final.1 = f32[512,64]{1,0:T(8,128)} custom-call(f32[128,128]{1,0:T(8,128)} %get-tuple-element.16.first_keep, f32[128,128]{1,0:T(8,128)} %copy-done.7, f32[128,128]{1,0:T(8,128)} %get-tuple-element.14.second_keep, f32[128,128]{1,0:T(8,128)} %copy-done.6), custom_call_target="tpu_custom_call" | custom-call | tf_op jit(solution)/shard_map/final/pallas_call | solution.py:306
  95.9 1.7 %copy.11 = f32[512,64]{0,1:T(8,128)} copy(f32[512,64]{1,0:T(8,128)} %final.1) | data formatting | bytes 262144 | tf_op jit(solution)/shard_map/final/pallas_call | solution.py:306
  (24 shorter events, 0.2 us)
Async XLA Ops:
  0.0 5.7 %copy-start = (s32[8,64]{1,0:T(8,128)S(1)}, s32[8,64]{1,0:T(8,128)}, u32[]{:S(2)}) copy-start(s32[8,64]{1,0:T(8,128)} %param.14) | copy-start | bytes 6148
  1.3 12.4 %copy-start.1 = (f32[3,8,64,128]{3,2,1,0:T(8,128)}, f32[3,8,64,128]{3,2,1,0:T(8,128)S(1)}, u32[]{:S(2)}) copy-start(f32[3,8,64,128]{3,2,1,0:T(8,128)S(1)} %convert_multiply_fusion.own_ref) | copy-start | bytes 2359300
  1.3 12.3 %collective-permute-start.1 = (f32[3,8,64,128]{3,2,1,0:T(8,128)S(1)}, f32[3,8,64,128]{3,2,1,0:T(8,128)S(1)}, u32[]{:S(2)}, u32[]{:S(2)}) collective-permute-start(f32[3,8,64,128]{3,2,1,0:T(8,128)S(1)} %convert_multiply_fusion.own_ref), channel_id=1, source_target_pairs={{1,0},{2,1},{3,2},{4,3},{5,4},{6,5},{7,6},{8,7},{9,8},{10,9},{11,1... | collective-permute-start | bytes 2359304 | tf_op jit(solution)/shard_map/ppermute | solution.py:258
  2.6 11.0 %collective-permute-start = (f32[3,8,64,128]{3,2,1,0:T(8,128)S(1)}, f32[3,8,64,128]{3,2,1,0:T(8,128)S(1)}, u32[]{:S(2)}, u32[]{:S(2)}) collective-permute-start(f32[3,8,64,128]{3,2,1,0:T(8,128)S(1)} %convert_multiply_fusion.own_ref), channel_id=1, source_target_pairs={{0,1},{1,2},{2,3},{3,4},{4,5},{5,6},{6,7},{7,8},{8,9},{9,10},{10,1... | collective-permute-start | bytes 2359304 | tf_op jit(solution)/shard_map/ppermute | solution.py:257
  13.6 0.9 copy-start.4
  13.6 1.1 %copy-start.5 = (f32[3,8,64,128]{3,2,1,0:T(8,128)}, f32[3,8,64,128]{3,2,1,0:T(8,128)S(1)}, u32[]{:S(2)}) copy-start(f32[3,8,64,128]{3,2,1,0:T(8,128)S(1)} %collective-permute-done.before_ref) | copy-start | bytes 2359300
  53.2 12.0 %copy-start.2 = (f32[2048,128]{1,0:T(8,128)S(1)}, f32[2048,128]{1,0:T(8,128)}, u32[]{:S(2)}) copy-start(f32[2048,128]{1,0:T(8,128)} %get-tuple-element.11) | copy-start | bytes 3145732
  53.2 13.5 %copy-start.3 = (f32[2048,128]{1,0:T(8,128)S(1)}, f32[2048,128]{1,0:T(8,128)}, u32[]{:S(2)}) copy-start(f32[2048,128]{1,0:T(8,128)} %get-tuple-element.12) | copy-start | bytes 3145732
  54.5 12.3 %collective-permute-start.6 = (f32[1024,128]{1,0:T(8,128)S(1)}, f32[1024,128]{1,0:T(8,128)S(1)}, u32[]{:S(2)}, u32[]{:S(2)}) collective-permute-start(f32[1024,128]{1,0:T(8,128)S(1)} %slice.57), channel_id=1, source_target_pairs={{0,1},{1,0},{2,3},{3,2},{4,5},{5,4},{6,7},{7,6},{8,9},{9,8},{10,11... | collective-permute-start | bytes 1572872 | tf_op jit(solution)/shard_map/ppermute | solution.py:298
  65.3 3.3 %collective-permute-start.2 = (f32[1024,128]{1,0:T(8,128)S(1)}, f32[1024,128]{1,0:T(8,128)S(1)}, u32[]{:S(2)}, u32[]{:S(2)}) collective-permute-start(f32[1024,128]{1,0:T(8,128)S(1)} %slice.49), channel_id=1, source_target_pairs={{0,1},{1,0},{2,3},{3,2},{4,5},{5,4},{6,7},{7,6},{8,9},{9,8},{10,11... | collective-permute-start | bytes 1572872 | tf_op jit(solution)/shard_map/ppermute | solution.py:298
  66.8 8.7 %collective-permute-start.7 = (f32[512,128]{1,0:T(8,128)S(1)}, f32[512,128]{1,0:T(8,128)S(1)}, u32[]{:S(2)}, u32[]{:S(2)}) collective-permute-start(f32[512,128]{1,0:T(8,128)S(1)} %slice.71), channel_id=1, source_target_pairs={{0,4},{1,5},{2,6},{3,7},{4,0},{5,1},{6,2},{7,3},{8,12},{9,13},{10,... | collective-permute-start | bytes 786440 | tf_op jit(solution)/shard_map/ppermute | solution.py:298
  68.7 9.6 %collective-permute-start.3 = (f32[512,128]{1,0:T(8,128)S(1)}, f32[512,128]{1,0:T(8,128)S(1)}, u32[]{:S(2)}, u32[]{:S(2)}) collective-permute-start(f32[512,128]{1,0:T(8,128)S(1)} %slice.65), channel_id=1, source_target_pairs={{0,2},{1,3},{2,0},{3,1},{4,6},{5,7},{6,4},{7,5},{8,10},{9,11},{10,... | collective-permute-start | bytes 786440 | tf_op jit(solution)/shard_map/ppermute | solution.py:298
  75.5 8.8 %collective-permute-start.8 = (f32[256,128]{1,0:T(8,128)S(1)}, f32[256,128]{1,0:T(8,128)S(1)}, u32[]{:S(2)}, u32[]{:S(2)}) collective-permute-start(f32[256,128]{1,0:T(8,128)S(1)} %slice.73), channel_id=1, source_target_pairs={{0,8},{1,9},{2,10},{3,11},{4,12},{5,13},{6,14},{7,15},{8,0},{9,1},... | collective-permute-start | bytes 393224 | tf_op jit(solution)/shard_map/ppermute | solution.py:298
  78.3 8.8 %collective-permute-start.4 = (f32[256,128]{1,0:T(8,128)S(1)}, f32[256,128]{1,0:T(8,128)S(1)}, u32[]{:S(2)}, u32[]{:S(2)}) collective-permute-start(f32[256,128]{1,0:T(8,128)S(1)} %slice.67), channel_id=1, source_target_pairs={{0,4},{1,5},{2,6},{3,7},{4,0},{5,1},{6,2},{7,3},{8,12},{9,13},{10,... | collective-permute-start | bytes 393224 | tf_op jit(solution)/shard_map/ppermute | solution.py:298
  85.0 4.4 %collective-permute-start.9 = (f32[128,128]{1,0:T(8,128)S(1)}, f32[128,128]{1,0:T(8,128)S(1)}, u32[]{:S(2)}, u32[]{:S(2)}) collective-permute-start(f32[128,128]{1,0:T(8,128)S(1)} %get-tuple-element.13), channel_id=1, source_target_pairs={{0,2},{1,3},{2,0},{3,1},{4,6},{5,7},{6,4},{7,5},{8,10},{9,11},{10,... | collective-permute-start | bytes 196616 | tf_op jit(solution)/shard_map/ppermute | solution.py:298
  87.8 5.5 %collective-permute-start.5 = (f32[128,128]{1,0:T(8,128)S(1)}, f32[128,128]{1,0:T(8,128)S(1)}, u32[]{:S(2)}, u32[]{:S(2)}) collective-permute-start(f32[128,128]{1,0:T(8,128)S(1)} %get-tuple-element.15), channel_id=1, source_target_pairs={{0,8},{1,9},{2,10},{3,11},{4,12},{5,13},{6,14},{7,15},{8,0},{9,1},... | collective-permute-start | bytes 196616 | tf_op jit(solution)/shard_map/ppermute | solution.py:298
  89.4 4.0 %copy-start.6 = (f32[128,128]{1,0:T(8,128)}, f32[128,128]{1,0:T(8,128)S(1)}, u32[]{:S(2)}) copy-start(f32[128,128]{1,0:T(8,128)S(1)} %collective-permute-done.9.second_got) | copy-start | bytes 196612
  93.3 0.6 copy-start.7
where the time goes:
time: 97.9 us; the launch traced here: 97.6 us
  Pallas kernels  47.7 us (49%)
  starting transfers between devices  27.4 us (28%)
  waiting for transfers between devices  14.2 us (15%)
  local copies, waits for them, and re-layouts  6.68 us (7%)
  other arithmetic  1.47 us (2%)
    pallas_call x1, Pallas kernels, shards(): pl.pallas_call(functools.partial(main_kernel, copies), out_shape=(table_s...  38.5 us
    ppermute x8, starting transfers between devices, exchange(): return (value[:middle], lax.ppermute(value[middle:], 'xy', pairs))  23.1 us
    ppermute x8, waiting for transfers between devices, exchange(): return (value[:middle], lax.ppermute(value[middle:], 'xy', pairs))  14.2 us
    pallas_call x1, Pallas kernels, shards(): pl.pallas_call(functools.partial(index_kernel, owners, rows_owned, height...  7.31 us
    ppermute x1, starting transfers between devices, shards(): before = lax.ppermute(dequant[:, planes - HALO:], 'xy', up)  3.08 us
    slice x8, local copies, waits for them, and re-layouts, exchange(): return (value[:middle], lax.ppermute(value[middle:], 'xy', pairs))  2.59 us
  transfers between devices with their start and end apart: 10, of which 5 were waited for; matrix products, arithmetic and copies ran while one was open for 2% of the time, Pallas kernels for 7%

commit v1 on v0

v1 whole, which is shorter than its diff:
```python
import functools

import jax
import jax.numpy as jnp
import numpy as np
from jax import lax
from jax.experimental import pallas as pl
from jax.experimental.pallas import tpu as pltpu
from jax.sharding import PartitionSpec as P

SLOTS = 8
HALO = 8
FEAT = 64
LANES = 128

sigma_list = (0.8, 1.3, 2.0, 3.0)
SCALES = len(sigma_list)
RESP = 3 * SCALES
ROWS = 2 * RESP + 2 * RESP + 8


def taps(sigma):
    offsets = np.arange(-HALO, HALO + 1).astype(np.float32)
    weights = np.exp(-offsets * offsets / np.float32(2.0 * sigma * sigma)).astype(np.float32)
    return (weights / weights.sum(dtype=np.float32)).astype(np.float32)


def band(weights, length):
    rows = np.arange(length)[:, None]
    cols = np.arange(length)[None, :]
    offset = cols - rows + HALO
    inside = (offset >= 0) & (offset <= 2 * HALO)
    return np.where(inside, weights[np.clip(offset, 0, 2 * HALO)], 0.0).astype(np.float32)


def halves(value):
    high = value.astype(jnp.bfloat16)
    low = (value - high.astype(jnp.float32)).astype(jnp.bfloat16)
    return high, low


def constant_halves(value):
    high = value.astype(jnp.bfloat16)
    low = (value - high.astype(np.float32)).astype(jnp.bfloat16)
    return high, low


def filter_constants(height, depth):
    along_y, along_z = [], []
    for sigma in sigma_list:
        high, low = constant_halves(band(taps(sigma), depth).T)
        along_y.append(np.concatenate([high, high, low], 0))
        high, low = constant_halves(band(taps(sigma), height))
        along_z.append(np.concatenate([high, high, low], 1))
    return np.stack(along_y), np.stack(along_z)


def order_bits(owners):
    bits = owners.bit_length() - 1
    first = list(range(bits))
    return first, [0] + first[2:] + first[1:2]


def index_kernel(owners, rows_owned, height, me_ref, edge_ref, count_ref, home_ref, target_ref):
    lists = edge_ref[...]
    both = jnp.concatenate([lists, lists], 1)
    high = both // LANES
    low = both % LANES

    def pick(row, found):
        line = jnp.broadcast_to(home_ref[pl.ds(row, 1), :], both.shape)
        return jnp.where(high == row, jnp.take_along_axis(line, low, axis=1), found)

    home = lax.fori_loop(0, home_ref.shape[0], pick, jnp.zeros(both.shape, jnp.int32))[:, :height]
    entry = lax.broadcasted_iota(jnp.int32, home.shape, 0)
    slot = entry % SLOTS
    owner = (home // rows_owned) ^ me_ref[0]
    within = home % rows_owned
    quarter = rows_owned // 4
    part = within // (2 * quarter)
    first, second = order_bits(owners)
    bits = len(first)
    place_first = jnp.zeros_like(owner)
    place_second = jnp.zeros_like(owner)
    for position in range(bits):
        place_first += ((owner >> first[position]) & 1) << (bits - 1 - position)
        place_second += ((owner >> second[position]) & 1) << (bits - 1 - position)
    place = jnp.where(part == 0, place_first, owners + place_second)
    row = place * (2 * quarter) + within % (2 * quarter)
    valid = slot < count_ref[...]
    target_ref[...] = jnp.where(valid, row, owners * rows_owned)


def main_kernel(
    copies, quarter, before_ref, own_ref, after_ref, slots_ref, y_ref, z_ref, target_ref, keep_ref, send_ref, *scratch
):
    blurred, fields, entries = scratch[:3]
    tables = scratch[3:]
    planes, height, depth = own_ref.shape[1:]
    half = height // 2
    weights = [[float(w) for w in taps(sigma)] for sigma in sigma_list]
    tiles = height // 8

    def across(step, carry):
        channel = step // tiles
        rows = pl.ds(pl.multiple_of(step % tiles * 8, 8), 8)
        values = [before_ref[channel, planes - HALO + p, rows, :] for p in range(HALO)]
        values += [own_ref[channel, p, rows, :] for p in range(planes)]
        values += [after_ref[channel, p, rows, :] for p in range(HALO)]
        for q in range(planes):
            center = q + HALO
            sums = [values[center]] + [values[center - t] + values[center + t] for t in range(1, HALO + 1)]
            for scale in range(SCALES):
                total = sums[0] * weights[scale][HALO]
                for t in range(1, HALO + 1):
                    total = total + sums[t] * weights[scale][HALO + t]
                blurred[scale * 3 + channel, q, rows, :] = total
        return carry

    lax.fori_loop(0, 3 * tiles, across, 0)

    def put(row_first, row_second, value):
        for q in range(planes):
            for b, row in enumerate((row_first, row_second)):
                start = q * half * ROWS + row
                fields[pl.ds(start, half, stride=ROWS), :] = value[b * half : (b + 1) * half, q * LANES : (q + 1) * LANES]

    def put_resp(number, value):
        put(number, 16 + number if number < 8 else 4 + number, value)

    def put_other(number, value):
        put(2 * RESP + number, 2 * RESP + 16 + number, value)

    for scale in range(SCALES):
        results = []
        for channel in range(3):
            high, low = halves(blurred[scale * 3 + channel].reshape(planes * height, depth))
            line = jnp.dot(jnp.concatenate([high, low, high], 1), y_ref[scale], preferred_element_type=jnp.float32)
            high, low = halves(line)
            high, low = high.reshape(planes, height, depth), low.reshape(planes, height, depth)
            stacked = jnp.concatenate([high, low, high], 1)
            side_by_side = jnp.concatenate([stacked[q] for q in range(planes)], 1)
            result = jnp.dot(z_ref[scale], side_by_side, preferred_element_type=jnp.float32)
            put_resp(scale * 3 + channel, result)
            results.append(result)
        for number, (a, b) in enumerate(((0, 1), (0, 2), (1, 2))):
            put_other(scale * 3 + number, results[a] * results[b])
    for channel in range(3):
        put_other(RESP + channel, jnp.concatenate([own_ref[channel, q] for q in range(planes)], 1))
    put_other(RESP + 3, jnp.ones((height, planes * LANES), jnp.float32))

    sub = lax.broadcasted_iota(jnp.int32, (SLOTS, LANES), 0)
    group = 8
    steps = planes * half // group

    def block_sums(step, carry):
        plane = step // (half // group)
        base = step % (half // group) * group
        parts = []
        for g in range(group):
            zz = base + g
            tile = fields[pl.ds(pl.multiple_of((plane * half + zz) * ROWS, 8), ROWS), :]
            powers = []
            for piece in range(3):
                resp = tile[8 * piece : 8 * piece + 8]
                square = resp * resp
                powers.append((resp, square, square * resp, square * square))
            shared = powers[1]
            shifted = [pltpu.roll(value, 4, 0) for value in shared]
            mixed = [
                [jnp.where(sub < 4, shared[k], shifted[k + 1]) for k in (0, 2)],
                [jnp.where(sub < 4, shifted[k], shared[k + 1]) for k in (0, 2)],
            ]
            highs, lows = [], []
            for b in range(2):
                other = tile[2 * RESP + 16 * b : 2 * RESP + 16 * b + 16]
                high, low = halves(jnp.concatenate([*powers[2 * b], *mixed[b], other], 0))
                highs.append(high)
                lows.append(low)
            upper = (slots_ref[plane, pl.ds(zz, 1), :] == sub).astype(jnp.float32)
            lower = (slots_ref[plane, pl.ds(zz + half, 1), :] == sub).astype(jnp.float32)
            none = jnp.zeros_like(upper)
            hot = jnp.concatenate([jnp.concatenate([upper, none], 0), jnp.concatenate([none, lower], 0)], 1)
            hot = hot.astype(jnp.bfloat16)
            dims = (((1,), (1,)), ((), ()))
            parts.append(
                lax.dot_general(
                    jnp.concatenate(highs + lows, 1), jnp.concatenate([hot, hot], 1), dims, preferred_element_type=jnp.float32
                )
            )
        sums = jnp.concatenate(parts, 1)
        start = pl.multiple_of(step * (group * 2 * SLOTS), group * 2 * SLOTS)
        entries[pl.ds(start, group * 2 * SLOTS), :] = jnp.concatenate([sums, sums], 0).T
        for table in tables:
            rows = table.shape[0] // steps // 8 * 8
            table[pl.ds(pl.multiple_of(step * rows, 8), rows), :] = jnp.zeros((rows, LANES), jnp.float32)
        return carry

    lax.fori_loop(0, steps, block_sums, 0)

    def scatter(step, carry):
        base = step // SLOTS * (height * SLOTS) + step % SLOTS
        for column in range(height):
            table = tables[column % copies]
            target = pl.ds(target_ref[step, column], 1)
            source = pl.ds(base + (column % half * 2 + column // half) * SLOTS, 1)
            table[target, :] = table[target, :] + entries[source, :]
        return carry

    lax.fori_loop(0, planes * SLOTS, scatter, 0)

    kept = keep_ref.shape[0]
    places = kept // (2 * quarter)
    left = lax.broadcasted_iota(jnp.int32, (quarter, LANES), 1) < FEAT

    def combine(step, carry):
        for part in range(2):
            for out, first in ((keep_ref, 0), (send_ref, places)):
                row = pl.multiple_of((part * 2 * places + first + step) * 2 * quarter, 2 * quarter)
                total = tables[0][pl.ds(row, 2 * quarter), :]
                for table in tables[1:]:
                    total = total + table[pl.ds(row, 2 * quarter), :]
                place = pl.multiple_of((part * places + step) * quarter, quarter)
                out[pl.ds(place, quarter), :] = jnp.where(left, total[:quarter], total[quarter:])
        return carry

    lax.fori_loop(0, places, combine, 0)


def final_kernel(first_keep, first_got, second_keep, second_got, out_ref):
    quarter = first_keep.shape[0]
    moves = [(8 * k, 12 * k, 8) for k in range(4)] + [(32 + 4 * k, 12 * k + 8, 4) for k in range(4)] + [(48, 48, 16)]
    for number, (keep, got) in enumerate(((first_keep, first_got), (second_keep, second_got))):
        table = (keep[...] + got[...]).T
        for side in range(2):
            rows = table[side * FEAT : (side + 1) * FEAT]
            count = rows[FEAT - 1 :]
            lane = lax.broadcasted_iota(jnp.int32, rows.shape, 0)
            result = jnp.where(lane == FEAT - 1, jnp.log(1.0 + rows), rows / jnp.maximum(count, 1.0))
            columns = pl.ds((2 * number + side) * quarter, quarter)
            for source, target, length in moves:
                out_ref[target : target + length, columns] = result[source : source + length]


def shards(affinity, block_scale, slot_map, edge_list, valid_count, edge_home):
    planes, height, depth = affinity.shape[1:]
    owners = lax.axis_size("xy")
    rows_owned = edge_home.shape[0] // owners
    quarter = rows_owned // 4
    vmem = pl.BlockSpec(memory_space=pltpu.VMEM)
    smem = pl.BlockSpec(memory_space=pltpu.SMEM)

    dequant = affinity.astype(jnp.float32) * block_scale[..., None]
    up = [(i, i + 1) for i in range(owners - 1)]
    down = [(j, i) for i, j in up]
    before = lax.ppermute(dequant[:, planes - HALO :], "xy", up)
    after = lax.ppermute(dequant[:, :HALO], "xy", down)

    me = lax.axis_index("xy").astype(jnp.int32).reshape(1)
    lists = edge_list.transpose(0, 2, 1).reshape(planes * SLOTS, height)
    counts = jnp.broadcast_to(valid_count[:, None, :], (planes, SLOTS, height)).reshape(planes * SLOTS, height)
    index_shape = jax.ShapeDtypeStruct((planes * SLOTS, height), jnp.int32)
    target = pl.pallas_call(
        functools.partial(index_kernel, owners, rows_owned, height),
        out_shape=jax.ShapeDtypeStruct((planes * SLOTS, height), jnp.int32),
        in_specs=[smem, vmem, vmem, vmem],
        out_specs=vmem,
        name="index",
    )(me, lists, counts, edge_home.reshape(-1, LANES))

    along_y, along_z = filter_constants(height, depth)
    table_rows = owners * rows_owned
    copies = 4 if table_rows <= 8192 else 1
    table_shape = jax.ShapeDtypeStruct((owners * quarter, LANES), jnp.float32)
    keep, send = pl.pallas_call(
        functools.partial(main_kernel, copies, quarter),
        out_shape=(table_shape, table_shape),
        in_specs=[vmem] * 6 + [smem],
        out_specs=(vmem, vmem),
        scratch_shapes=[
            pltpu.VMEM((RESP, planes, height, depth), jnp.float32),
            pltpu.VMEM((planes * (height // 2) * ROWS, LANES), jnp.float32),
            pltpu.VMEM((planes * height * SLOTS, LANES), jnp.float32),
        ]
        + [pltpu.VMEM((table_rows + 8, LANES), jnp.float32)] * copies,
        compiler_params=pltpu.CompilerParams(vmem_limit_bytes=58 << 20),
        name="features",
    )(before, dequant, after, slot_map, jnp.asarray(along_y), jnp.asarray(along_z), target)

    def swap(value, bit):
        return lax.ppermute(value, "xy", [(i, i ^ (1 << bit)) for i in range(owners)])

    order_first, order_second = order_bits(owners)
    table = keep + swap(send, 0)
    first, second = table[: owners // 2 * quarter], table[owners // 2 * quarter :]
    for bit_first, bit_second in zip(order_first[1:], order_second[1:]):
        middle = first.shape[0] // 2
        got_first, got_second = swap(first[middle:], bit_first), swap(second[middle:], bit_second)
        first, second = first[:middle], second[:middle]
        if middle > quarter:
            first, second = first + got_first, second + got_second
    out = pl.pallas_call(
        final_kernel,
        out_shape=jax.ShapeDtypeStruct((FEAT, rows_owned), jnp.float32),
        in_specs=[vmem] * 4,
        out_specs=vmem,
        name="final",
    )(first, got_first, second, got_second)
    return out.T


def solution(mesh):
    in_specs = (
        P(None, ("parts", "xy"), None, None),
        P(None, ("parts", "xy"), None),
        P(("parts", "xy"), None, None),
        P(("parts", "xy"), None, None),
        P(("parts", "xy"), None),
        P("parts"),
    )
    out_specs = P(("parts", "xy"), None)
    return jax.shard_map(shards, mesh=mesh, in_specs=in_specs, out_specs=out_specs, check_vma=False)
```

time: 97.9 us -> 94.5 us (0.965)
  waiting for transfers between devices: 14.2 us -> 21 us
  Pallas kernels: 47.7 us -> 41.1 us
  starting transfers between devices: 27.4 us -> 25 us
  local copies, waits for them, and re-layouts: 6.68 us -> 4.32 us
  other arithmetic: 1.47 us -> 2.73 us
    ppermute x8 -> x7, waiting for transfers between devices: 14.2 us -> 21 us  [swap(): return lax.ppermute(value, 'xy', [(i, i ^ 1 << bit) for i in range(owners)])]
    pallas_call x2, Pallas kernels: 40.4 us -> 33.8 us  [the longest x1 32.1 us: shards(): pl.pallas_call(functools.partial(main_kernel, copies, quarter), out_shape...]
    ppermute x8 -> x7, starting transfers between devices: 23.1 us -> 20.6 us  [swap(): return lax.ppermute(value, 'xy', [(i, i ^ 1 << bit) for i in range(owners)])]
    pallas_call x1 -> x0, local copies, waits for them, and re-layouts: 1.72 us -> none  [shards(): pl.pallas_call(final_kernel, out_shape=jax.ShapeDtypeStruct((rows_owned,...]
    slice x8 -> x5, local copies, waits for them, and re-layouts: 2.59 us -> 1.32 us  [the longest x3 0.67 us: shards(): second[middle:]]
    add x6 -> x5, other arithmetic: 0.2 us -> 1.45 us  [the longest x1 1.33 us: shards(): table = keep + swap(send, 0)]
    unnamed x16 -> x12, local copies, waits for them, and re-layouts: 1.75 us -> 2.38 us
  transfers between devices with their start and end apart: 10 -> 9, of which waited for: 5 -> 6; matrix products, arithmetic and copies ran while one was open for 2% -> 2% of each run, Pallas kernels for 7% -> 8%
where the time goes in v1:
time: 94.5 us; the launch traced here: 94.2 us
  Pallas kernels  41.1 us (43%)
  starting transfers between devices  25 us (26%)
  waiting for transfers between devices  21 us (22%)
  local copies, waits for them, and re-layouts  4.32 us (5%)
  other arithmetic  2.73 us (3%)
    pallas_call x1, Pallas kernels, shards(): pl.pallas_call(functools.partial(main_kernel, copies, quarter), out_shape...  32.1 us
    ppermute x7, waiting for transfers between devices, swap(): return lax.ppermute(value, 'xy', [(i, i ^ 1 << bit) for i in range(owners)])  21 us
    ppermute x7, starting transfers between devices, swap(): return lax.ppermute(value, 'xy', [(i, i ^ 1 << bit) for i in range(owners)])  20.6 us
    pallas_call x1, Pallas kernels, shards(): pl.pallas_call(functools.partial(index_kernel, owners, rows_owned, height...  7.29 us
    ppermute x1, starting transfers between devices, shards(): before = lax.ppermute(dequant[:, planes - HALO:], 'xy', up)  3.08 us
    unnamed x12, local copies, waits for them, and re-layouts  2.38 us
  transfers between devices with their start and end apart: 9, of which 6 were waited for; matrix products, arithmetic and copies ran while one was open for 2% of the time, Pallas kernels for 8%

profile of v1, /device:TPU:0, one launch (start us, length us, event | category | flops | bytes accessed | tf_op | source)
XLA Modules:
  0.0 94.2 jit_solution(647803305608393598)
XLA Ops:
  0.0 0.0 copy-start
  0.0 1.3 %convert_multiply_fusion.own_ref = f32[3,8,64,128]{3,2,1,0:T(8,128)S(1)} fusion(bf16[3,8,64,128]{3,2,1,0:T(8,128)(2,1)} %param.8, f32[3,8,64]{2,1,0:T(8,128)} %param.9), kind=kLoop, calls=%fused_computation | loop fusion | flops 393216 | bytes 1185792 | tf_op jit(solution)/shard_map/mul | solution.py:253
  1.3 0.0 copy-start.1
  1.3 1.3 %collective-permute-start.1 = (f32[3,8,64,128]{3,2,1,0:T(8,128)S(1)}, f32[3,8,64,128]{3,2,1,0:T(8,128)S(1)}, u32[]{:S(2)}, u32[]{:S(2)}) collective-permute-start(f32[3,8,64,128]{3,2,1,0:T(8,128)S(1)} %convert_multiply_fusion.own_ref), channel_id=1, source_target_pairs={{1,0},{2,1},{3,2},{4,3},{5,4},{6,5},{7,6},{8,7},{9,8},{10,9},{11,1... | collective-permute-start | bytes 2359304 | tf_op jit(solution)/shard_map/ppermute | solution.py:257
  2.6 3.1 %collective-permute-start = (f32[3,8,64,128]{3,2,1,0:T(8,128)S(1)}, f32[3,8,64,128]{3,2,1,0:T(8,128)S(1)}, u32[]{:S(2)}, u32[]{:S(2)}) collective-permute-start(f32[3,8,64,128]{3,2,1,0:T(8,128)S(1)} %convert_multiply_fusion.own_ref), channel_id=1, source_target_pairs={{0,1},{1,2},{2,3},{3,4},{4,5},{5,6},{6,7},{7,8},{8,9},{9,10},{10,1... | collective-permute-start | bytes 2359304 | tf_op jit(solution)/shard_map/ppermute | solution.py:256
  5.7 0.6 broadcast_bitcast_fusion.count_ref
  6.3 7.3 %index.1.target_ref = s32[64,64]{1,0:T(8,128)} custom-call(s32[1]{0:T(128)} %bitcast.me_ref, s32[64,64]{1,0:T(8,128)} %bitcast.8, s32[64,64]{1,0:T(8,128)} %broadcast_bitcast_fusion.count_ref, s32[64,128]{1,0:T(8,128)} %bitcast.9), custom_call_target="tpu_custom_call" | custom-call | tf_op jit(solution)/shard_map/index/pallas_call | solution.py:263
  13.6 0.0 collective-permute-done.1.after_ref
  13.6 0.0 collective-permute-done.before_ref
  13.6 0.9 copy-done.2
  14.5 0.9 copy-done.3
  15.4 32.1 %features.1 = (f32[2048,128]{1,0:T(8,128)}, f32[2048,128]{1,0:T(8,128)}) custom-call(f32[3,8,64,128]{3,2,1,0:T(8,128)} %copy-done.3, f32[3,8,64,128]{3,2,1,0:T(8,128)} %copy-done.1, f32[3,8,64,128]{3,2,1,0:T(8,128)} %copy-done.2, s32[8,64,128]{2,1,0:T(8,128)} %slots_ref.1, bf16[4,384,128]{2,1,0:T(8,128)(2,1)} %constant.8.clone.y_ref, ...), custom_call_target="tpu_custom_call" | custom-call | tf_op jit(solution)/shard_map/features/pallas_call | solution.py:275
  47.4 10.0 %collective-permute-start.2 = (f32[2048,128]{1,0:T(8,128)}, f32[2048,128]{1,0:T(8,128)S(1)}, u32[]{:S(2)}, u32[]{:S(2)}) collective-permute-start(f32[2048,128]{1,0:T(8,128)} %get-tuple-element.8), channel_id=1, source_target_pairs={{0,1},{1,0},{2,3},{3,2},{4,5},{5,4},{6,7},{7,6},{8,9},{9,8},{10,11... | collective-permute-start | bytes 3145736 | tf_op jit(solution)/shard_map/ppermute | solution.py:291
  57.5 2.5 %collective-permute-done.2 = f32[2048,128]{1,0:T(8,128)S(1)} collective-permute-done((f32[2048,128]{1,0:T(8,128)}, f32[2048,128]{1,0:T(8,128)S(1)}, u32[]{:S(2)}, u32[]{:S(2)}) %collective-permute-start.2) | collective-permute-done | bytes 1048608 | tf_op jit(solution)/shard_map/ppermute | solution.py:291
  60.0 1.3 %add.15 = f32[2048,128]{1,0:T(8,128)S(1)} add(f32[2048,128]{1,0:T(8,128)} %get-tuple-element.7, f32[2048,128]{1,0:T(8,128)S(1)} %collective-permute-done.2) | non-fusion elementwise | flops 262144 | bytes 3145728 | tf_op jit(solution)/shard_map/add | solution.py:294
  61.4 2.4 %collective-permute-start.6 = (f32[512,128]{1,0:T(8,128)S(1)}, f32[512,128]{1,0:T(8,128)S(1)}, u32[]{:S(2)}, u32[]{:S(2)}) collective-permute-start(f32[512,128]{1,0:T(8,128)S(1)} %slice.61), channel_id=1, source_target_pairs={{0,4},{1,5},{2,6},{3,7},{4,0},{5,1},{6,2},{7,3},{8,12},{9,13},{10,... | collective-permute-start | bytes 786440 | tf_op jit(solution)/shard_map/ppermute | solution.py:291
  63.7 6.8 %collective-permute-done.6 = f32[512,128]{1,0:T(8,128)S(1)} collective-permute-done((f32[512,128]{1,0:T(8,128)S(1)}, f32[512,128]{1,0:T(8,128)S(1)}, u32[]{:S(2)}, u32[]{:S(2)}) %collective-permute-start.6) | collective-permute-done | bytes 262176 | tf_op jit(solution)/shard_map/ppermute | solution.py:291
  70.6 0.1 slice_add_fusion
  70.6 2.9 %collective-permute-start.7 = (f32[256,128]{1,0:T(8,128)S(1)}, f32[256,128]{1,0:T(8,128)S(1)}, u32[]{:S(2)}, u32[]{:S(2)}) collective-permute-start(f32[256,128]{1,0:T(8,128)S(1)} %slice.63), channel_id=1, source_target_pairs={{0,8},{1,9},{2,10},{3,11},{4,12},{5,13},{6,14},{7,15},{8,0},{9,1},... | collective-permute-start | bytes 393224 | tf_op jit(solution)/shard_map/ppermute | solution.py:291
  73.5 1.8 %collective-permute-start.3 = (f32[512,128]{1,0:T(8,128)S(1)}, f32[512,128]{1,0:T(8,128)S(1)}, u32[]{:S(2)}, u32[]{:S(2)}) collective-permute-start(f32[512,128]{1,0:T(8,128)S(1)} %get-tuple-element.10), channel_id=1, source_target_pairs={{0,2},{1,3},{2,0},{3,1},{4,6},{5,7},{6,4},{7,5},{8,10},{9,11},{10,... | collective-permute-start | bytes 786440 | tf_op jit(solution)/shard_map/ppermute | solution.py:291
  75.3 4.3 %collective-permute-done.7 = f32[256,128]{1,0:T(8,128)S(1)} collective-permute-done((f32[256,128]{1,0:T(8,128)S(1)}, f32[256,128]{1,0:T(8,128)S(1)}, u32[]{:S(2)}, u32[]{:S(2)}) %collective-permute-start.7) | collective-permute-done | bytes 131104 | tf_op jit(solution)/shard_map/ppermute | solution.py:291
  79.6 1.3 %collective-permute-done.3 = f32[512,128]{1,0:T(8,128)S(1)} collective-permute-done((f32[512,128]{1,0:T(8,128)S(1)}, f32[512,128]{1,0:T(8,128)S(1)}, u32[]{:S(2)}, u32[]{:S(2)}) %collective-permute-start.3) | collective-permute-done | bytes 262176 | tf_op jit(solution)/shard_map/ppermute | solution.py:291
  81.0 1.6 %collective-permute-start.4 = (f32[256,128]{1,0:T(8,128)S(1)}, f32[256,128]{1,0:T(8,128)S(1)}, u32[]{:S(2)}, u32[]{:S(2)}) collective-permute-start(f32[256,128]{1,0:T(8,128)S(1)} %slice.57), channel_id=1, source_target_pairs={{0,4},{1,5},{2,6},{3,7},{4,0},{5,1},{6,2},{7,3},{8,12},{9,13},{10,... | collective-permute-start | bytes 393224 | tf_op jit(solution)/shard_map/ppermute | solution.py:291
  82.6 0.6 fusion
  83.2 0.6 collective-permute-start.8
  83.8 2.2 %collective-permute-done.4 = f32[256,128]{1,0:T(8,128)S(1)} collective-permute-done((f32[256,128]{1,0:T(8,128)S(1)}, f32[256,128]{1,0:T(8,128)S(1)}, u32[]{:S(2)}, u32[]{:S(2)}) %collective-permute-start.4) | collective-permute-done | bytes 131104 | tf_op jit(solution)/shard_map/ppermute | solution.py:291
  86.0 0.6 fusion.1
  86.7 1.4 %collective-permute-start.5 = (f32[128,128]{1,0:T(8,128)S(1)}, f32[128,128]{1,0:T(8,128)S(1)}, u32[]{:S(2)}, u32[]{:S(2)}) collective-permute-start(f32[128,128]{1,0:T(8,128)S(1)} %get-tuple-element.13), channel_id=1, source_target_pairs={{0,8},{1,9},{2,10},{3,11},{4,12},{5,13},{6,14},{7,15},{8,0},{9,1},... | collective-permute-start | bytes 196616 | tf_op jit(solution)/shard_map/ppermute | solution.py:291
  88.1 0.0 collective-permute-done.8.second_got
  88.1 3.8 %collective-permute-done.5.first_got = f32[128,128]{1,0:T(8,128)S(1)} collective-permute-done((f32[128,128]{1,0:T(8,128)S(1)}, f32[128,128]{1,0:T(8,128)S(1)}, u32[]{:S(2)}, u32[]{:S(2)}) %collective-permute-start.5) | collective-permute-done | bytes 65568 | tf_op jit(solution)/shard_map/ppermute | solution.py:291
  91.9 0.6 copy-done.5
  92.5 1.7 %final.1 = f32[64,512]{1,0:T(8,128)} custom-call(f32[128,128]{1,0:T(8,128)} %get-tuple-element.14.first_keep, f32[128,128]{1,0:T(8,128)} %copy-done.5, f32[128,128]{1,0:T(8,128)} %get-tuple-element.12.second_keep, f32[128,128]{1,0:T(8,128)} %copy-done.4), custom_call_target="tpu_custom_call" | custom-call | tf_op jit(solution)/shard_map/final/pallas_call | solution.py:302
  (13 shorter events, 0.1 us)
Async XLA Ops:
  0.0 5.7 %copy-start = (s32[8,64]{1,0:T(8,128)S(1)}, s32[8,64]{1,0:T(8,128)}, u32[]{:S(2)}) copy-start(s32[8,64]{1,0:T(8,128)} %param.12) | copy-start | bytes 6148
  1.3 12.3 %copy-start.1 = (f32[3,8,64,128]{3,2,1,0:T(8,128)}, f32[3,8,64,128]{3,2,1,0:T(8,128)S(1)}, u32[]{:S(2)}) copy-start(f32[3,8,64,128]{3,2,1,0:T(8,128)S(1)} %convert_multiply_fusion.own_ref) | copy-start | bytes 2359300
  1.3 12.3 %collective-permute-start.1 = (f32[3,8,64,128]{3,2,1,0:T(8,128)S(1)}, f32[3,8,64,128]{3,2,1,0:T(8,128)S(1)}, u32[]{:S(2)}, u32[]{:S(2)}) collective-permute-start(f32[3,8,64,128]{3,2,1,0:T(8,128)S(1)} %convert_multiply_fusion.own_ref), channel_id=1, source_target_pairs={{1,0},{2,1},{3,2},{4,3},{5,4},{6,5},{7,6},{8,7},{9,8},{10,9},{11,1... | collective-permute-start | bytes 2359304 | tf_op jit(solution)/shard_map/ppermute | solution.py:257
  2.6 11.0 %collective-permute-start = (f32[3,8,64,128]{3,2,1,0:T(8,128)S(1)}, f32[3,8,64,128]{3,2,1,0:T(8,128)S(1)}, u32[]{:S(2)}, u32[]{:S(2)}) collective-permute-start(f32[3,8,64,128]{3,2,1,0:T(8,128)S(1)} %convert_multiply_fusion.own_ref), channel_id=1, source_target_pairs={{0,1},{1,2},{2,3},{3,4},{4,5},{5,6},{6,7},{7,8},{8,9},{9,10},{10,1... | collective-permute-start | bytes 2359304 | tf_op jit(solution)/shard_map/ppermute | solution.py:256
  13.6 0.9 copy-start.2
  14.5 0.9 copy-start.3
  47.4 12.5 %collective-permute-start.2 = (f32[2048,128]{1,0:T(8,128)}, f32[2048,128]{1,0:T(8,128)S(1)}, u32[]{:S(2)}, u32[]{:S(2)}) collective-permute-start(f32[2048,128]{1,0:T(8,128)} %get-tuple-element.8), channel_id=1, source_target_pairs={{0,1},{1,0},{2,3},{3,2},{4,5},{5,4},{6,7},{7,6},{8,9},{9,8},{10,11... | collective-permute-start | bytes 3145736 | tf_op jit(solution)/shard_map/ppermute | solution.py:291
  61.4 9.2 %collective-permute-start.6 = (f32[512,128]{1,0:T(8,128)S(1)}, f32[512,128]{1,0:T(8,128)S(1)}, u32[]{:S(2)}, u32[]{:S(2)}) collective-permute-start(f32[512,128]{1,0:T(8,128)S(1)} %slice.61), channel_id=1, source_target_pairs={{0,4},{1,5},{2,6},{3,7},{4,0},{5,1},{6,2},{7,3},{8,12},{9,13},{10,... | collective-permute-start | bytes 786440 | tf_op jit(solution)/shard_map/ppermute | solution.py:291
  70.6 9.0 %collective-permute-start.7 = (f32[256,128]{1,0:T(8,128)S(1)}, f32[256,128]{1,0:T(8,128)S(1)}, u32[]{:S(2)}, u32[]{:S(2)}) collective-permute-start(f32[256,128]{1,0:T(8,128)S(1)} %slice.63), channel_id=1, source_target_pairs={{0,8},{1,9},{2,10},{3,11},{4,12},{5,13},{6,14},{7,15},{8,0},{9,1},... | collective-permute-start | bytes 393224 | tf_op jit(solution)/shard_map/ppermute | solution.py:291
  73.5 7.4 %collective-permute-start.3 = (f32[512,128]{1,0:T(8,128)S(1)}, f32[512,128]{1,0:T(8,128)S(1)}, u32[]{:S(2)}, u32[]{:S(2)}) collective-permute-start(f32[512,128]{1,0:T(8,128)S(1)} %get-tuple-element.10), channel_id=1, source_target_pairs={{0,2},{1,3},{2,0},{3,1},{4,6},{5,7},{6,4},{7,5},{8,10},{9,11},{10,... | collective-permute-start | bytes 786440 | tf_op jit(solution)/shard_map/ppermute | solution.py:291
  81.0 5.0 %collective-permute-start.4 = (f32[256,128]{1,0:T(8,128)S(1)}, f32[256,128]{1,0:T(8,128)S(1)}, u32[]{:S(2)}, u32[]{:S(2)}) collective-permute-start(f32[256,128]{1,0:T(8,128)S(1)} %slice.57), channel_id=1, source_target_pairs={{0,4},{1,5},{2,6},{3,7},{4,0},{5,1},{6,2},{7,3},{8,12},{9,13},{10,... | collective-permute-start | bytes 393224 | tf_op jit(solution)/shard_map/ppermute | solution.py:291
  83.2 4.8 %collective-permute-start.8 = (f32[128,128]{1,0:T(8,128)S(1)}, f32[128,128]{1,0:T(8,128)S(1)}, u32[]{:S(2)}, u32[]{:S(2)}) collective-permute-start(f32[128,128]{1,0:T(8,128)S(1)} %get-tuple-element.11), channel_id=1, source_target_pairs={{0,2},{1,3},{2,0},{3,1},{4,6},{5,7},{6,4},{7,5},{8,10},{9,11},{10,... | collective-permute-start | bytes 196616 | tf_op jit(solution)/shard_map/ppermute | solution.py:291
  86.7 5.2 %collective-permute-start.5 = (f32[128,128]{1,0:T(8,128)S(1)}, f32[128,128]{1,0:T(8,128)S(1)}, u32[]{:S(2)}, u32[]{:S(2)}) collective-permute-start(f32[128,128]{1,0:T(8,128)S(1)} %get-tuple-element.13), channel_id=1, source_target_pairs={{0,8},{1,9},{2,10},{3,11},{4,12},{5,13},{6,14},{7,15},{8,0},{9,1},... | collective-permute-start | bytes 196616 | tf_op jit(solution)/shard_map/ppermute | solution.py:291
  88.1 3.8 %copy-start.4 = (f32[128,128]{1,0:T(8,128)}, f32[128,128]{1,0:T(8,128)S(1)}, u32[]{:S(2)}) copy-start(f32[128,128]{1,0:T(8,128)S(1)} %collective-permute-done.8.second_got) | copy-start | bytes 196612
  91.9 0.6 copy-start.5

commit v2 on v1

--- a/solution.py
+++ b/solution.py
@@ -49,7 +49,7 @@
     along_y, along_z = [], []
     for sigma in sigma_list:
         high, low = constant_halves(band(taps(sigma), depth).T)
-        along_y.append(np.concatenate([high, high, low], 0))
+        along_y.append(np.concatenate([np.concatenate([high, low], 1), np.concatenate([high, np.zeros_like(low)], 1)], 0))
         high, low = constant_halves(band(taps(sigma), height))
         along_z.append(np.concatenate([high, high, low], 1))
     return np.stack(along_y), np.stack(along_z)
@@ -94,12 +94,13 @@
 def main_kernel(
     copies, quarter, before_ref, own_ref, after_ref, slots_ref, y_ref, z_ref, target_ref, keep_ref, send_ref, *scratch
 ):
-    blurred, fields, entries = scratch[:3]
-    tables = scratch[3:]
+    blurred, fields, pending, entries = scratch[:4]
+    tables = scratch[4:]
     planes, height, depth = own_ref.shape[1:]
     half = height // 2
     weights = [[float(w) for w in taps(sigma)] for sigma in sigma_list]
     tiles = height // 8
+    cleared = tables[0].shape[0] // (3 * tiles)
 
     def across(step, carry):
         channel = step // tiles
@@ -115,6 +116,8 @@
                 for t in range(1, HALO + 1):
                     total = total + sums[t] * weights[scale][HALO + t]
                 blurred[scale * 3 + channel, q, rows, :] = total
+        for table in tables:
+            table[pl.ds(pl.multiple_of(step * cleared, 8), cleared), :] = jnp.zeros((cleared, LANES), jnp.float32)
         return carry
 
     lax.fori_loop(0, 3 * tiles, across, 0)
@@ -132,17 +135,16 @@
         put(2 * RESP + number, 2 * RESP + 16 + number, value)
 
     for scale in range(SCALES):
-        results = []
+        high, low = halves(blurred[3 * scale : 3 * scale + 3].reshape(3 * planes * height, depth))
+        line = jnp.dot(jnp.concatenate([high, low], 1), y_ref[scale], preferred_element_type=jnp.float32)
+        high, low = halves(line[:, :depth] + line[:, depth:])
+        high, low = high.reshape(3 * planes, height, depth), low.reshape(3 * planes, height, depth)
+        stacked = jnp.concatenate([high, low, high], 1)
+        side_by_side = jnp.concatenate([stacked[p] for p in range(3 * planes)], 1)
+        result = jnp.dot(z_ref[scale], side_by_side, preferred_element_type=jnp.float32)
+        results = [result[:, c * planes * depth : (c + 1) * planes * depth] for c in range(3)]
         for channel in range(3):
-            high, low = halves(blurred[scale * 3 + channel].reshape(planes * height, depth))
-            line = jnp.dot(jnp.concatenate([high, low, high], 1), y_ref[scale], preferred_element_type=jnp.float32)
-            high, low = halves(line)
-            high, low = high.reshape(planes, height, depth), low.reshape(planes, height, depth)
-            stacked = jnp.concatenate([high, low, high], 1)
-            side_by_side = jnp.concatenate([stacked[q] for q in range(planes)], 1)
-            result = jnp.dot(z_ref[scale], side_by_side, preferred_element_type=jnp.float32)
-            put_resp(scale * 3 + channel, result)
-            results.append(result)
+            put_resp(scale * 3 + channel, results[channel])
         for number, (a, b) in enumerate(((0, 1), (0, 2), (1, 2))):
             put_other(scale * 3 + number, results[a] * results[b])
     for channel in range(3):
@@ -150,13 +152,26 @@
     put_other(RESP + 3, jnp.ones((height, planes * LANES), jnp.float32))
 
     sub = lax.broadcasted_iota(jnp.int32, (SLOTS, LANES), 0)
-    group = 8
+    group = LANES // (2 * SLOTS)
+    owner_lane = lax.broadcasted_iota(jnp.int32, (FEAT, LANES), 1) // (2 * SLOTS)
     steps = planes * half // group
 
-    def block_sums(step, carry):
+    def scatter(step):
+        for number in range(LANES):
+            table = tables[number % copies]
+            target = pl.ds(target_ref[step, number], 1)
+            table[target, :] = table[target, :] + entries[number : number + 1, :]
+
+    def turn():
+        sums = pending[...]
+        entries[...] = jnp.concatenate([sums, sums], 0).T
+
+    def block_sums(step):
+        scatter(step)
+        turn()
         plane = step // (half // group)
         base = step % (half // group) * group
-        parts = []
+        parts, hots = [], []
         for g in range(group):
             zz = base + g
             tile = fields[pl.ds(pl.multiple_of((plane * half + zz) * ROWS, 8), ROWS), :]
@@ -180,34 +195,28 @@
             upper = (slots_ref[plane, pl.ds(zz, 1), :] == sub).astype(jnp.float32)
             lower = (slots_ref[plane, pl.ds(zz + half, 1), :] == sub).astype(jnp.float32)
             none = jnp.zeros_like(upper)
-            hot = jnp.concatenate([jnp.concatenate([upper, none], 0), jnp.concatenate([none, lower], 0)], 1)
-            hot = hot.astype(jnp.bfloat16)
-            dims = (((1,), (1,)), ((), ()))
-            parts.append(
-                lax.dot_general(
-                    jnp.concatenate(highs + lows, 1), jnp.concatenate([hot, hot], 1), dims, preferred_element_type=jnp.float32
-                )
-            )
-        sums = jnp.concatenate(parts, 1)
-        start = pl.multiple_of(step * (group * 2 * SLOTS), group * 2 * SLOTS)
-        entries[pl.ds(start, group * 2 * SLOTS), :] = jnp.concatenate([sums, sums], 0).T
-        for table in tables:
-            rows = table.shape[0] // steps // 8 * 8
-            table[pl.ds(pl.multiple_of(step * rows, 8), rows), :] = jnp.zeros((rows, LANES), jnp.float32)
+            hots += [jnp.concatenate([upper, none], 1), jnp.concatenate([none, lower], 1)]
+            parts += [jnp.concatenate(highs, 1), jnp.concatenate(lows, 1)]
+        hot = jnp.concatenate(hots, 0).astype(jnp.bfloat16)
+        dims = (((1,), (1,)), ((), ()))
+        products = lax.dot_general(jnp.concatenate(parts, 0), hot, dims, preferred_element_type=jnp.float32)
+        sums = jnp.zeros((FEAT, LANES), jnp.float32)
+        for g in range(group):
+            own = products[2 * g * FEAT : (2 * g + 1) * FEAT] + products[(2 * g + 1) * FEAT : (2 * g + 2) * FEAT]
+            sums = jnp.where(owner_lane == g, own, sums)
+        pending[...] = sums
+
+    unroll = 2 if steps % 2 == 0 else 1
+
+    def several(step, carry):
+        for number in range(unroll):
+            block_sums(step * unroll + number)
         return carry
 
-    lax.fori_loop(0, steps, block_sums, 0)
-
-    def scatter(step, carry):
-        base = step // SLOTS * (height * SLOTS) + step % SLOTS
-        for column in range(height):
-            table = tables[column % copies]
-            target = pl.ds(target_ref[step, column], 1)
-            source = pl.ds(base + (column % half * 2 + column // half) * SLOTS, 1)
-            table[target, :] = table[target, :] + entries[source, :]
-        return carry
-
-    lax.fori_loop(0, planes * SLOTS, scatter, 0)
+    lax.fori_loop(0, steps // unroll, several, 0)
+    scatter(steps)
+    turn()
+    scatter(steps + 1)
 
     kept = keep_ref.shape[0]
     places = kept // (2 * quarter)
@@ -227,19 +236,40 @@
     lax.fori_loop(0, places, combine, 0)
 
 
-def final_kernel(first_keep, first_got, second_keep, second_got, out_ref):
-    quarter = first_keep.shape[0]
+def add_kernel(layers, *refs):
+    ins, outs = refs[:-2], refs[-2:]
+    count = len(ins) // 2
+    for number, out in enumerate(outs):
+        total = None
+        for ref, start in zip(ins[number * count : (number + 1) * count], layers[number]):
+            piece = ref[start : start + out.shape[0], :]
+            total = piece if total is None else total + piece
+        out[...] = total
+
+
+def final_kernel(layers, *refs):
+    ins, out_ref = refs[:-1], refs[-1]
+    count = len(ins) // 2
+    quarter = ins[count - 1].shape[0]
     moves = [(8 * k, 12 * k, 8) for k in range(4)] + [(32 + 4 * k, 12 * k + 8, 4) for k in range(4)] + [(48, 48, 16)]
-    for number, (keep, got) in enumerate(((first_keep, first_got), (second_keep, second_got))):
-        table = (keep[...] + got[...]).T
+    for number in range(2):
+        table = None
+        for ref, start in zip(ins[number * count : (number + 1) * count], layers[number]):
+            piece = ref[start : start + quarter, :]
+            table = piece if table is None else table + piece
+        table = table.T
         for side in range(2):
             rows = table[side * FEAT : (side + 1) * FEAT]
-            count = rows[FEAT - 1 :]
+            count_row = rows[FEAT - 1 :]
             lane = lax.broadcasted_iota(jnp.int32, rows.shape, 0)
-            result = jnp.where(lane == FEAT - 1, jnp.log(1.0 + rows), rows / jnp.maximum(count, 1.0))
+            result = jnp.where(lane == FEAT - 1, jnp.log(1.0 + rows), rows / jnp.maximum(count_row, 1.0))
             columns = pl.ds((2 * number + side) * quarter, quarter)
             for source, target, length in moves:
                 out_ref[target : target + length, columns] = result[source : source + length]
+
+
+def on_chip(value):
+    return pltpu.with_memory_space_constraint(value, pltpu.VMEM)
 
 
 def shards(affinity, block_scale, slot_map, edge_list, valid_count, edge_home):
@@ -253,8 +283,8 @@
     dequant = affinity.astype(jnp.float32) * block_scale[..., None]
     up = [(i, i + 1) for i in range(owners - 1)]
     down = [(j, i) for i, j in up]
-    before = lax.ppermute(dequant[:, planes - HALO :], "xy", up)
-    after = lax.ppermute(dequant[:, :HALO], "xy", down)
+    before = on_chip(lax.ppermute(dequant[:, planes - HALO :], "xy", up))
+    after = on_chip(lax.ppermute(dequant[:, :HALO], "xy", down))
 
     me = lax.axis_index("xy").astype(jnp.int32).reshape(1)
     lists = edge_list.transpose(0, 2, 1).reshape(planes * SLOTS, height)
@@ -268,9 +298,14 @@
         name="index",
     )(me, lists, counts, edge_home.reshape(-1, LANES))
 
+    target = target.reshape(planes, SLOTS, 2, height // 2).transpose(0, 3, 2, 1).reshape(-1, LANES)
+    target = jnp.pad(target, ((2, 0), (0, 0)), constant_values=owners * rows_owned)
+
     along_y, along_z = filter_constants(height, depth)
     table_rows = owners * rows_owned
     copies = 4 if table_rows <= 8192 else 1
+    clear_steps = 3 * height // 8
+    cleared = -(-(table_rows + 8) // (8 * clear_steps)) * 8
     table_shape = jax.ShapeDtypeStruct((owners * quarter, LANES), jnp.float32)
     keep, send = pl.pallas_call(
         functools.partial(main_kernel, copies, quarter),
@@ -280,32 +315,47 @@
         scratch_shapes=[
             pltpu.VMEM((RESP, planes, height, depth), jnp.float32),
             pltpu.VMEM((planes * (height // 2) * ROWS, LANES), jnp.float32),
-            pltpu.VMEM((planes * height * SLOTS, LANES), jnp.float32),
+            pltpu.VMEM((FEAT, LANES), jnp.float32),
+            pltpu.VMEM((LANES, LANES), jnp.float32),
         ]
-        + [pltpu.VMEM((table_rows + 8, LANES), jnp.float32)] * copies,
-        compiler_params=pltpu.CompilerParams(vmem_limit_bytes=58 << 20),
+        + [pltpu.VMEM((clear_steps * cleared, LANES), jnp.float32)] * copies,
+        compiler_params=pltpu.CompilerParams(vmem_limit_bytes=44 << 20),
         name="features",
-    )(before, dequant, after, slot_map, jnp.asarray(along_y), jnp.asarray(along_z), target)
+    )(before, on_chip(dequant), after, slot_map, jnp.asarray(along_y), jnp.asarray(along_z), target)
+
+    small = table_rows <= 8192
+    near = on_chip if small else lambda value: value
 
     def swap(value, bit):
-        return lax.ppermute(value, "xy", [(i, i ^ (1 << bit)) for i in range(owners)])
+        return near(lax.ppermute(value, "xy", [(i, i ^ (1 << bit)) for i in range(owners)]))
 
     order_first, order_second = order_bits(owners)
-    table = keep + swap(send, 0)
-    first, second = table[: owners // 2 * quarter], table[owners // 2 * quarter :]
+    whole = owners // 2 * quarter
+    got = swap(send, 0)
+    keep = near(keep)
+    first, second = [keep, got], [keep, got]
+    starts = ([0, 0], [whole, whole])
+    middle = whole
     for bit_first, bit_second in zip(order_first[1:], order_second[1:]):
-        middle = first.shape[0] // 2
-        got_first, got_second = swap(first[middle:], bit_first), swap(second[middle:], bit_second)
-        first, second = first[:middle], second[:middle]
-        if middle > quarter:
-            first, second = first + got_first, second + got_second
+        middle //= 2
+        layers = tuple(tuple(start + middle for start in part) for part in starts)
+        shape = jax.ShapeDtypeStruct((middle, LANES), jnp.float32)
+        send_first, send_second = pl.pallas_call(
+            functools.partial(add_kernel, layers),
+            out_shape=(shape, shape),
+            in_specs=[vmem] * (2 * len(first)),
+            out_specs=(vmem, vmem),
+            name="add",
+        )(*first, *second)
+        first, second = first + [swap(send_first, bit_first)], second + [swap(send_second, bit_second)]
+        starts = (starts[0] + [0], starts[1] + [0])
     out = pl.pallas_call(
-        final_kernel,
+        functools.partial(final_kernel, starts),
         out_shape=jax.ShapeDtypeStruct((FEAT, rows_owned), jnp.float32),
-        in_specs=[vmem] * 4,
+        in_specs=[vmem] * (2 * len(first)),
         out_specs=vmem,
         name="final",
-    )(first, got_first, second, got_second)
+    )(*first, *second)
     return out.T
 
 

time: 94.5 us -> 76 us (0.80)
  Pallas kernels: 41.1 us -> 27.2 us
  starting transfers between devices: 25 us -> 20.7 us
  other arithmetic: 2.73 us -> 1.28 us
  local copies, waits for them, and re-layouts: 4.32 us -> 5.36 us
    pallas_call x1, Pallas kernels: 32.1 us -> 16.8 us  [shards(): pl.pallas_call(functools.partial(main_kernel, copies, quarter), out_shape...]
    ppermute x9, starting transfers between devices: 25 us -> 20.7 us  [the longest x7 16.2 us: swap(): lax.ppermute(value, 'xy', [(i, i ^ 1 << bit) for i in range(owners)])]
    reshape x0 -> x3, local copies, waits for them, and re-layouts: none -> 1.98 us  [shards(): target.reshape(planes, SLOTS, 2, height // 2).transpose(0, 3, 2, 1)]
    add x5 -> x0, other arithmetic: 1.45 us -> none  [the longest x1 1.33 us: shards(): table = keep + swap(send, 0)]
    pallas_call x1 -> x4, Pallas kernels: 1.7 us -> 3.07 us  [the longest x3 2.29 us: shards(): pl.pallas_call(functools.partial(add_kernel, layers), out_shape=(shape, s...]
    slice x5 -> x0, local copies, waits for them, and re-layouts: 1.32 us -> none  [the longest x3 0.67 us: shards(): second[middle:]]
  transfers between devices with their start and end apart: 9 -> 9, of which waited for: 6 -> 6; matrix products, arithmetic and copies ran while one was open for 2% -> 4% of each run, Pallas kernels for 8% -> 10%
where the time goes in v2:
time: 76 us; the launch traced here: 75.6 us
  Pallas kernels  27.2 us (36%)
  waiting for transfers between devices  21 us (28%)
  starting transfers between devices  20.7 us (27%)
  local copies, waits for them, and re-layouts  5.36 us (7%)
  other arithmetic  1.28 us (2%)
    ppermute x7, waiting for transfers between devices, swap(): lax.ppermute(value, 'xy', [(i, i ^ 1 << bit) for i in range(owners)])  21 us
    pallas_call x1, Pallas kernels, shards(): pl.pallas_call(functools.partial(main_kernel, copies, quarter), out_shape...  16.8 us
    ppermute x7, starting transfers between devices, swap(): lax.ppermute(value, 'xy', [(i, i ^ 1 << bit) for i in range(owners)])  16.2 us
    pallas_call x1, Pallas kernels, shards(): pl.pallas_call(functools.partial(index_kernel, owners, rows_owned, height...  7.29 us
    ppermute x1, starting transfers between devices, shards(): before = on_chip(lax.ppermute(dequant[:, planes - HALO:], 'xy', up))  3.08 us
    pallas_call x3, Pallas kernels, shards(): pl.pallas_call(functools.partial(add_kernel, layers), out_shape=(shape, s...  2.29 us
    unnamed x12, local copies, waits for them, and re-layouts  2.04 us
    reshape x3, local copies, waits for them, and re-layouts, shards(): target.reshape(planes, SLOTS, 2, height // 2).transpose(0, 3, 2, 1)  1.98 us
  transfers between devices with their start and end apart: 9, of which 6 were waited for; matrix products, arithmetic and copies ran while one was open for 4% of the time, Pallas kernels for 10%

profile of v2, /device:TPU:0, one launch (start us, length us, event | category | flops | bytes accessed | tf_op | source)
XLA Modules:
  0.0 75.6 jit_solution(4388083476824713609)
XLA Ops:
  0.0 1.3 %convert_multiply_fusion.own_ref = f32[3,8,64,128]{3,2,1,0:T(8,128)S(1)} fusion(bf16[3,8,64,128]{3,2,1,0:T(8,128)(2,1)} %param.8, f32[3,8,64]{2,1,0:T(8,128)} %param.9), kind=kLoop, calls=%fused_computation | loop fusion | flops 393216 | bytes 1185792 | tf_op jit(solution)/shard_map/mul | solution.py:283
  1.3 0.0 copy-start.3
  1.3 1.4 %collective-permute-start.1 = (f32[3,8,64,128]{3,2,1,0:T(8,128)S(1)}, f32[3,8,64,128]{3,2,1,0:T(8,128)S(1)}, u32[]{:S(2)}, u32[]{:S(2)}) collective-permute-start(f32[3,8,64,128]{3,2,1,0:T(8,128)S(1)} %convert_multiply_fusion.own_ref), channel_id=1, source_target_pairs={{1,0},{2,1},{3,2},{4,3},{5,4},{6,5},{7,6},{8,7},{9,8},{10,9},{11,1... | collective-permute-start | bytes 2359304 | tf_op jit(solution)/shard_map/ppermute | solution.py:287
  2.7 3.1 %collective-permute-start = (f32[3,8,64,128]{3,2,1,0:T(8,128)S(1)}, f32[3,8,64,128]{3,2,1,0:T(8,128)S(1)}, u32[]{:S(2)}, u32[]{:S(2)}) collective-permute-start(f32[3,8,64,128]{3,2,1,0:T(8,128)S(1)} %convert_multiply_fusion.own_ref), channel_id=1, source_target_pairs={{0,1},{1,2},{2,3},{3,4},{4,5},{5,6},{6,7},{7,8},{8,9},{9,10},{10,1... | collective-permute-start | bytes 2359304 | tf_op jit(solution)/shard_map/ppermute | solution.py:286
  5.8 0.6 broadcast_bitcast_fusion.count_ref
  6.4 7.3 %index.1 = s32[64,64]{1,0:T(8,128)} custom-call(s32[1]{0:T(128)} %bitcast.me_ref, s32[64,64]{1,0:T(8,128)} %bitcast.10, s32[64,64]{1,0:T(8,128)} %broadcast_bitcast_fusion.count_ref, s32[64,128]{1,0:T(8,128)} %bitcast.11), custom_call_target="tpu_custom_call" | custom-call | tf_op jit(solution)/shard_map/index/pallas_call | solution.py:293
  13.7 0.9 %reshape.24 = s32[8,8,2,32]{3,2,1,0:T(2,128)S(1)} reshape(s32[64,64]{1,0:T(8,128)} %index.1) | data formatting | bytes 32768 | tf_op jit(solution)/shard_map/reshape | solution.py:301
  14.6 0.0 copy-start.4
  14.6 0.2 copy.10
  14.8 0.0 copy-start.5
  14.8 1.0 %reshape.25 = s32[32,128]{1,0:T(8,128)} reshape(s32[8,32,2,8]{3,2,1,0:T(2,128)S(1)} %bitcast.9) | data formatting | bytes 32768 | tf_op jit(solution)/shard_map/reshape | solution.py:301
  15.8 0.7 pad.4.target_ref
  16.5 0.9 %copy-done.1 = f32[3,8,64,128]{3,2,1,0:T(8,128)} copy-done((f32[3,8,64,128]{3,2,1,0:T(8,128)}, f32[3,8,64,128]{3,2,1,0:T(8,128)S(1)}, u32[]{:S(2)}) %copy-start.1) | copy-done | bytes 786456
  17.4 1.1 %copy-done.2 = f32[3,8,64,128]{3,2,1,0:T(8,128)S(1)} copy-done((f32[3,8,64,128]{3,2,1,0:T(8,128)S(1)}, f32[3,8,64,128]{3,2,1,0:T(8,128)}, u32[]{:S(2)}) %copy-start.2) | copy-done | bytes 786456
  18.5 16.8 %features.1 = (f32[2048,128]{1,0:T(8,128)S(1)}, f32[2048,128]{1,0:T(8,128)S(1)}) custom-call(f32[3,8,64,128]{3,2,1,0:T(8,128)S(1)} %copy-done.2, f32[3,8,64,128]{3,2,1,0:T(8,128)S(1)} %convert_multiply_fusion.own_ref, f32[3,8,64,128]{3,2,1,0:T(8,128)S(1)} %collective-permute-done.1.after_ref, s32[8,64,128]{2,1,0:T(8,128)S(1)} %copy-done.4, ...), custom_call_target="tpu_custom_call" | custom-call | tf_op jit(solution)/shard_map/features/pallas_call | solution.py:310
  35.4 8.3 %collective-permute-start.2 = (f32[2048,128]{1,0:T(8,128)S(1)}, f32[2048,128]{1,0:T(8,128)S(1)}, u32[]{:S(2)}, u32[]{:S(2)}) collective-permute-start(f32[2048,128]{1,0:T(8,128)S(1)} %get-tuple-element.14), channel_id=1, source_target_pairs={{0,1},{1,0},{2,3},{3,2},{4,5},{5,4},{6,7},{7,6},{8,9},{9,8},{10,11... | collective-permute-start | bytes 3145736 | tf_op jit(solution)/shard_map/ppermute | solution.py:330
  43.6 2.3 %collective-permute-done.2.refs_1_.refs_3_.refs_4_.refs_5_.refs_6_ = f32[2048,128]{1,0:T(8,128)S(1)} collective-permute-done((f32[2048,128]{1,0:T(8,128)S(1)}, f32[2048,128]{1,0:T(8,128)S(1)}, u32[]{:S(2)}, u32[]{:S(2)}) %collective-permute-start.2) | collective-permute-done | bytes 1048608 | tf_op jit(solution)/shard_map/ppermute | solution.py:330
  45.9 0.9 %add.5 = (f32[512,128]{1,0:T(8,128)}, f32[512,128]{1,0:T(8,128)}) custom-call(f32[2048,128]{1,0:T(8,128)S(1)} %get-tuple-element.13.refs_0_.refs_2_.refs_3_.refs_4_.refs_5_, f32[2048,128]{1,0:T(8,128)S(1)} %collective-permute-done.2.refs_1_.refs_3_.refs_4_.refs_5_.refs_6_, f32[2048,128]{1,0:T(8,128)S(1)} %get-tuple-element.13.refs_0_.refs_2_.refs_3_.refs_4_.refs_5_, ...), custom_call_target="tpu_custom_call" | custom-call | tf_op jit(solution)/shard_map/add/pallas_call | solution.py:343
  46.8 2.7 %collective-permute-start.3 = (f32[512,128]{1,0:T(8,128)}, f32[512,128]{1,0:T(8,128)S(1)}, u32[]{:S(2)}, u32[]{:S(2)}) collective-permute-start(f32[512,128]{1,0:T(8,128)} %get-tuple-element.15), channel_id=1, source_target_pairs={{0,2},{1,3},{2,0},{3,1},{4,6},{5,7},{6,4},{7,5},{8,10},{9,11},{10,... | collective-permute-start | bytes 786440 | tf_op jit(solution)/shard_map/ppermute | solution.py:330
  49.5 1.6 %collective-permute-start.4 = (f32[512,128]{1,0:T(8,128)}, f32[512,128]{1,0:T(8,128)S(1)}, u32[]{:S(2)}, u32[]{:S(2)}) collective-permute-start(f32[512,128]{1,0:T(8,128)} %get-tuple-element.16), channel_id=1, source_target_pairs={{0,4},{1,5},{2,6},{3,7},{4,0},{5,1},{6,2},{7,3},{8,12},{9,13},{10,... | collective-permute-start | bytes 786440 | tf_op jit(solution)/shard_map/ppermute | solution.py:330
  51.1 5.2 %collective-permute-done.3.refs_2_ = f32[512,128]{1,0:T(8,128)S(1)} collective-permute-done((f32[512,128]{1,0:T(8,128)}, f32[512,128]{1,0:T(8,128)S(1)}, u32[]{:S(2)}, u32[]{:S(2)}) %collective-permute-start.3) | collective-permute-done | bytes 262176 | tf_op jit(solution)/shard_map/ppermute | solution.py:330
  56.4 1.5 %collective-permute-done.4.refs_5_.refs_6_.refs_7_ = f32[512,128]{1,0:T(8,128)S(1)} collective-permute-done((f32[512,128]{1,0:T(8,128)}, f32[512,128]{1,0:T(8,128)S(1)}, u32[]{:S(2)}, u32[]{:S(2)}) %collective-permute-start.4) | collective-permute-done | bytes 262176 | tf_op jit(solution)/shard_map/ppermute | solution.py:330
  57.8 0.8 add.6
  58.6 1.6 %collective-permute-start.5 = (f32[256,128]{1,0:T(8,128)}, f32[256,128]{1,0:T(8,128)S(1)}, u32[]{:S(2)}, u32[]{:S(2)}) collective-permute-start(f32[256,128]{1,0:T(8,128)} %get-tuple-element.17), channel_id=1, source_target_pairs={{0,4},{1,5},{2,6},{3,7},{4,0},{5,1},{6,2},{7,3},{8,12},{9,13},{10,... | collective-permute-start | bytes 393224 | tf_op jit(solution)/shard_map/ppermute | solution.py:330
  60.1 1.3 %collective-permute-start.6 = (f32[256,128]{1,0:T(8,128)}, f32[256,128]{1,0:T(8,128)S(1)}, u32[]{:S(2)}, u32[]{:S(2)}) collective-permute-start(f32[256,128]{1,0:T(8,128)} %get-tuple-element.18), channel_id=1, source_target_pairs={{0,8},{1,9},{2,10},{3,11},{4,12},{5,13},{6,14},{7,15},{8,0},{9,1},... | collective-permute-start | bytes 393224 | tf_op jit(solution)/shard_map/ppermute | solution.py:330
  61.4 4.0 %collective-permute-done.5.refs_3_ = f32[256,128]{1,0:T(8,128)S(1)} collective-permute-done((f32[256,128]{1,0:T(8,128)}, f32[256,128]{1,0:T(8,128)S(1)}, u32[]{:S(2)}, u32[]{:S(2)}) %collective-permute-start.5) | collective-permute-done | bytes 131104 | tf_op jit(solution)/shard_map/ppermute | solution.py:330
  65.5 2.7 %collective-permute-done.6.refs_7_.refs_8_ = f32[256,128]{1,0:T(8,128)S(1)} collective-permute-done((f32[256,128]{1,0:T(8,128)}, f32[256,128]{1,0:T(8,128)S(1)}, u32[]{:S(2)}, u32[]{:S(2)}) %collective-permute-start.6) | collective-permute-done | bytes 131104 | tf_op jit(solution)/shard_map/ppermute | solution.py:330
  68.2 0.7 add.7
  68.9 0.3 collective-permute-start.7
  69.2 0.5 collective-permute-start.8
  69.7 5.2 %collective-permute-done.7.refs_4_ = f32[128,128]{1,0:T(8,128)S(1)} collective-permute-done((f32[128,128]{1,0:T(8,128)}, f32[128,128]{1,0:T(8,128)S(1)}, u32[]{:S(2)}, u32[]{:S(2)}) %collective-permute-start.7) | collective-permute-done | bytes 65568 | tf_op jit(solution)/shard_map/ppermute | solution.py:330
  74.9 0.8 %final.1 = f32[64,512]{1,0:T(8,128)} custom-call(f32[2048,128]{1,0:T(8,128)S(1)} %get-tuple-element.13.refs_0_.refs_2_.refs_3_.refs_4_.refs_5_, f32[2048,128]{1,0:T(8,128)S(1)} %collective-permute-done.2.refs_1_.refs_3_.refs_4_.refs_5_.refs_6_, f32[512,128]{1,0:T(8,128)S(1)} %collective-permute-done.3.refs_2_, ...), custom_call_target="tpu_custom_call" | custom-call | tf_op jit(solution)/shard_map/final/pallas_call | solution.py:352
  (10 shorter events, 0.0 us)
Async XLA Ops:
  0.0 5.8 %copy-start = (s32[8,64]{1,0:T(8,128)S(1)}, s32[8,64]{1,0:T(8,128)}, u32[]{:S(2)}) copy-start(s32[8,64]{1,0:T(8,128)} %param.12) | copy-start | bytes 6148
  1.3 16.1 %copy-start.3 = (bf16[4,256,256]{2,1,0:T(8,128)(2,1)S(1)}, bf16[4,256,256]{2,1,0:T(8,128)(2,1)}, u32[]{:S(2)}) copy-start(bf16[4,256,256]{2,1,0:T(8,128)(2,1)} %constant.10.clone.y_ref) | copy-start | bytes 1572868
  1.3 15.2 %collective-permute-start.1 = (f32[3,8,64,128]{3,2,1,0:T(8,128)S(1)}, f32[3,8,64,128]{3,2,1,0:T(8,128)S(1)}, u32[]{:S(2)}, u32[]{:S(2)}) collective-permute-start(f32[3,8,64,128]{3,2,1,0:T(8,128)S(1)} %convert_multiply_fusion.own_ref), channel_id=1, source_target_pairs={{1,0},{2,1},{3,2},{4,3},{5,4},{6,5},{7,6},{8,7},{9,8},{10,9},{11,1... | collective-permute-start | bytes 2359304 | tf_op jit(solution)/shard_map/ppermute | solution.py:287
  2.7 13.8 %collective-permute-start = (f32[3,8,64,128]{3,2,1,0:T(8,128)S(1)}, f32[3,8,64,128]{3,2,1,0:T(8,128)S(1)}, u32[]{:S(2)}, u32[]{:S(2)}) collective-permute-start(f32[3,8,64,128]{3,2,1,0:T(8,128)S(1)} %convert_multiply_fusion.own_ref), channel_id=1, source_target_pairs={{0,1},{1,2},{2,3},{3,4},{4,5},{5,6},{6,7},{7,8},{8,9},{9,10},{10,1... | collective-permute-start | bytes 2359304 | tf_op jit(solution)/shard_map/ppermute | solution.py:286
  14.6 2.8 %copy-start.4 = (s32[8,64,128]{2,1,0:T(8,128)S(1)}, s32[8,64,128]{2,1,0:T(8,128)}, u32[]{:S(2)}) copy-start(s32[8,64,128]{2,1,0:T(8,128)} %slots_ref.1) | copy-start | bytes 786436
  14.8 2.6 %copy-start.5 = (bf16[4,64,192]{2,1,0:T(8,128)(2,1)S(1)}, bf16[4,64,192]{2,1,0:T(8,128)(2,1)}, u32[]{:S(2)}) copy-start(bf16[4,64,192]{2,1,0:T(8,128)(2,1)} %constant.11.clone.z_ref) | copy-start | bytes 294916
  16.5 0.9 %copy-start.1 = (f32[3,8,64,128]{3,2,1,0:T(8,128)}, f32[3,8,64,128]{3,2,1,0:T(8,128)S(1)}, u32[]{:S(2)}) copy-start(f32[3,8,64,128]{3,2,1,0:T(8,128)S(1)} %collective-permute-done.before_ref) | copy-start | bytes 2359300
  17.4 1.1 %copy-start.2 = (f32[3,8,64,128]{3,2,1,0:T(8,128)S(1)}, f32[3,8,64,128]{3,2,1,0:T(8,128)}, u32[]{:S(2)}) copy-start(f32[3,8,64,128]{3,2,1,0:T(8,128)} %copy-done.1) | copy-start | bytes 2359300
  35.4 10.6 %collective-permute-start.2 = (f32[2048,128]{1,0:T(8,128)S(1)}, f32[2048,128]{1,0:T(8,128)S(1)}, u32[]{:S(2)}, u32[]{:S(2)}) collective-permute-start(f32[2048,128]{1,0:T(8,128)S(1)} %get-tuple-element.14), channel_id=1, source_target_pairs={{0,1},{1,0},{2,3},{3,2},{4,5},{5,4},{6,7},{7,6},{8,9},{9,8},{10,11... | collective-permute-start | bytes 3145736 | tf_op jit(solution)/shard_map/ppermute | solution.py:330
  46.8 9.6 %collective-permute-start.3 = (f32[512,128]{1,0:T(8,128)}, f32[512,128]{1,0:T(8,128)S(1)}, u32[]{:S(2)}, u32[]{:S(2)}) collective-permute-start(f32[512,128]{1,0:T(8,128)} %get-tuple-element.15), channel_id=1, source_target_pairs={{0,2},{1,3},{2,0},{3,1},{4,6},{5,7},{6,4},{7,5},{8,10},{9,11},{10,... | collective-permute-start | bytes 786440 | tf_op jit(solution)/shard_map/ppermute | solution.py:330
  49.5 8.3 %collective-permute-start.4 = (f32[512,128]{1,0:T(8,128)}, f32[512,128]{1,0:T(8,128)S(1)}, u32[]{:S(2)}, u32[]{:S(2)}) collective-permute-start(f32[512,128]{1,0:T(8,128)} %get-tuple-element.16), channel_id=1, source_target_pairs={{0,4},{1,5},{2,6},{3,7},{4,0},{5,1},{6,2},{7,3},{8,12},{9,13},{10,... | collective-permute-start | bytes 786440 | tf_op jit(solution)/shard_map/ppermute | solution.py:330
  58.6 6.9 %collective-permute-start.5 = (f32[256,128]{1,0:T(8,128)}, f32[256,128]{1,0:T(8,128)S(1)}, u32[]{:S(2)}, u32[]{:S(2)}) collective-permute-start(f32[256,128]{1,0:T(8,128)} %get-tuple-element.17), channel_id=1, source_target_pairs={{0,4},{1,5},{2,6},{3,7},{4,0},{5,1},{6,2},{7,3},{8,12},{9,13},{10,... | collective-permute-start | bytes 393224 | tf_op jit(solution)/shard_map/ppermute | solution.py:330
  60.1 8.1 %collective-permute-start.6 = (f32[256,128]{1,0:T(8,128)}, f32[256,128]{1,0:T(8,128)S(1)}, u32[]{:S(2)}, u32[]{:S(2)}) collective-permute-start(f32[256,128]{1,0:T(8,128)} %get-tuple-element.18), channel_id=1, source_target_pairs={{0,8},{1,9},{2,10},{3,11},{4,12},{5,13},{6,14},{7,15},{8,0},{9,1},... | collective-permute-start | bytes 393224 | tf_op jit(solution)/shard_map/ppermute | solution.py:330
  68.9 6.0 %collective-permute-start.7 = (f32[128,128]{1,0:T(8,128)}, f32[128,128]{1,0:T(8,128)S(1)}, u32[]{:S(2)}, u32[]{:S(2)}) collective-permute-start(f32[128,128]{1,0:T(8,128)} %get-tuple-element.19), channel_id=1, source_target_pairs={{0,8},{1,9},{2,10},{3,11},{4,12},{5,13},{6,14},{7,15},{8,0},{9,1},... | collective-permute-start | bytes 196616 | tf_op jit(solution)/shard_map/ppermute | solution.py:330
  69.2 5.6 %collective-permute-start.8 = (f32[128,128]{1,0:T(8,128)}, f32[128,128]{1,0:T(8,128)S(1)}, u32[]{:S(2)}, u32[]{:S(2)}) collective-permute-start(f32[128,128]{1,0:T(8,128)} %get-tuple-element.20), channel_id=1, source_target_pairs={{0,2},{1,3},{2,0},{3,1},{4,6},{5,7},{6,4},{7,5},{8,10},{9,11},{10,... | collective-permute-start | bytes 196616 | tf_op jit(solution)/shard_map/ppermute | solution.py:330
